TPU v7x, 32 devices: a whole 2x2x4 slice. The times are simulated.
32 devices in a mesh: half: 1, grp: 4 (over y, core), dev: 8 (over z, x).
Axes of the slice: x: 2, y: 2, z: 4, core: 2. Of those that a mesh axis runs over, the one named last changes fastest.
Arguments:
- panel_block: float32 [2048, 512], P(('half', 'grp', 'dev')), may hold values from -1 to 1, as said below
- trailing: float32 [2048, 1024], P(('half', 'grp'), 'dev'), may hold values from -6 to 6
Outputs:
- triangle: float32 [512, 512], replicated
- projected: float32 [512, 1024], P(None, 'dev')
- remainder: float32 [2048, 1024], P(('half', 'grp'), 'dev')
Inputs may be any that keep to these rules, and one draw needn't show every extreme that they name: `panel_block`: of full column rank.
All inputs are finite; a program needn't handle non-finite values.
Results may differ from a plain program's by a relative error of at most 0.0003.
Values sent between devices are 32-bit elements; how exact they have to be, the bound alone decides.
A program may use at most 64 MiB of HBM per device.

v0:
```python
import functools

import jax
import jax.numpy as jnp
from jax import lax
from jax.experimental import pallas as pl
from jax.experimental.pallas import tpu as pltpu
from jax.sharding import PartitionSpec as P

HIGHEST = lax.Precision.HIGHEST
NB = 128
SUB = 8


def dot(a, b):
    return jnp.dot(a, b, precision=HIGHEST, preferred_element_type=jnp.float32)


def dot_t(a, b):
    return lax.dot_general(
        a, b, (((0,), (0,)), ((), ())), precision=HIGHEST,
        preferred_element_type=jnp.float32,
    )


def factor_block(block, upper_ref, inverse_ref, row0, col0):
    tile = (SUB, NB)
    lane = lax.broadcasted_iota(jnp.int32, tile, 1)
    zero = jnp.zeros(tile, jnp.float32)
    groups = len(block)
    block = list(block)
    for b in range(groups):
        c0 = SUB * b
        own = block[b]
        marks = [lane == c0 + t for t in range(SUB)]
        inside = (lane >= c0) & (lane < c0 + SUB)
        after = lane >= c0 + SUB
        rows = [jnp.broadcast_to(own[s:s + 1, :], tile) for s in range(SUB)]
        d = {}
        for s in range(SUB):
            for t in range(s, SUB):
                d[s, t] = jnp.broadcast_to(rows[s][:, c0 + t:c0 + t + 1], tile)
        columns = [
            [jnp.broadcast_to(block[g][:, c0 + t:c0 + t + 1], tile) for t in range(SUB)]
            for g in range(b + 1, groups)
        ]
        v = []
        for s in range(SUB):
            unit = jnp.where(marks[s], 1.0, 0.0)
            v.append(jnp.where(inside, unit, rows[s]))
        for j in range(SUB):
            rs = lax.rsqrt(d[j, j])
            u = {k: d[j, k] * rs for k in range(j, SUB)}
            vs = v[j] * rs
            up = jnp.where(after, vs, zero)
            for k in range(j, SUB):
                up = jnp.where(marks[k], u[k], up)
            low = jnp.where(after, zero, vs)
            upper_ref[row0 + c0 + j:row0 + c0 + j + 1, col0:col0 + NB] = up[0:1, :]
            inverse_ref[row0 + c0 + j:row0 + c0 + j + 1, :] = low[0:1, :]
            for i in range(SUB):
                if i == j:
                    continue
                e = u[i] if i > j else d[i, j] * rs
                v[i] = v[i] - e * vs
                for k in range(max(j + 1, i), SUB):
                    d[i, k] = d[i, k] - e * u[k]
            v[j] = vs * rs
            for k in range(j + 1, SUB):
                d[j, k] = u[k] * rs
        for g in range(b + 1, groups):
            terms = [columns[g - b - 1][t] * v[t] for t in range(SUB)]
            while len(terms) > 1:
                terms = [terms[i] + terms[i + 1] for i in range(0, len(terms), 2)]
            block[g] = jnp.where(inside, zero, block[g]) - terms[0]


def solve_kernel(panel_ref, packed_ref, trailing_ref, triangle_ref, projected_ref,
                 remainder_ref, gram, cross, inverse, solved, corner, upper, lower):
    p = panel_ref.shape[1]
    blocks = p // NB
    for (i, j), at in packing(p, trailing_ref.shape[1]).items():
        part = packed_ref[at:at + NB, :]
        if j < blocks:
            gram[i * NB:(i + 1) * NB, j * NB:(j + 1) * NB] = part
        else:
            cross[i * NB:(i + 1) * NB, (j - blocks) * NB:(j - blocks + 1) * NB] = part
    def step(index, carry):
        start = pl.multiple_of(index * NB, NB)
        corner[...] = gram[pl.ds(start, NB), pl.ds(start, NB)]
        rows = [corner[SUB * g:SUB * (g + 1), :] for g in range(NB // SUB)]
        factor_block(rows, upper, lower, 0, 0)
        for k in range(blocks):
            pl.when(index == k)(functools.partial(update, k))
        return carry

    def update(k):
        a, z = k * NB, (k + 1) * NB
        w = lower[...]
        inverse[a:z, :] = w
        triangle_ref[a:z, a:z] = upper[...]
        if k:
            triangle_ref[a:z, 0:a] = jnp.zeros((NB, a), jnp.float32)
        if k + 1 < blocks:
            triangle_ref[a:z, z:p] = dot(w, gram[a:z, z:p])
        projected_ref[a:z, :] = dot(w, cross[a:z, :])
        for i in range(k + 1, blocks):
            lo, hi = i * NB, (i + 1) * NB
            left = triangle_ref[a:z, lo:hi]
            gram[lo:hi, lo:p] -= dot_t(left, triangle_ref[a:z, lo:p])
            cross[lo:hi, :] -= dot_t(left, projected_ref[a:z, :])

    lax.fori_loop(0, blocks, step, 0)
    for k in reversed(range(blocks)):
        a, z = k * NB, (k + 1) * NB
        rhs = projected_ref[a:z, :]
        if k + 1 < blocks:
            rhs = rhs - dot(triangle_ref[a:z, z:p], solved[z:p, :])
        solved[a:z, :] = dot_t(inverse[a:z, :], rhs)
    remainder_ref[...] = trailing_ref[...] - dot(panel_ref[...], solved[...])


def solve(panel_group, packed, trailing):
    p = panel_group.shape[1]
    n = trailing.shape[1]
    f32 = jnp.float32
    vmem = pl.BlockSpec(memory_space=pltpu.VMEM)
    return pl.pallas_call(
        solve_kernel,
        out_shape=(
            jax.ShapeDtypeStruct((p, p), f32),
            jax.ShapeDtypeStruct((p, n), f32),
            jax.ShapeDtypeStruct(trailing.shape, f32),
        ),
        in_specs=[vmem] * 3,
        out_specs=(vmem,) * 3,
        scratch_shapes=[
            pltpu.VMEM((p, p), f32),
            pltpu.VMEM((p, n), f32),
            pltpu.VMEM((p, NB), f32),
            pltpu.VMEM((p, n), f32),
            pltpu.VMEM((NB, NB), f32),
            pltpu.VMEM((NB, NB), f32),
            pltpu.VMEM((NB, NB), f32),
        ],
        name="factor_project",
    )(panel_group, packed, trailing)


def packing(p, n):
    blocks = p // NB
    where = {}
    for i in range(blocks):
        for j in range(i, blocks):
            where[i, j] = len(where) * NB
    for i in range(blocks):
        for j in range(n // NB):
            where[i, blocks + j] = len(where) * NB
    return where


def gather_kernel(halves, groups, devs, panel_ref, trailing_ref, group_ref, packed_ref, panel,
                  total, inbox, a_send, a_recv, b_send, b_recv, r_send, r_recv):
    mesh_ids = pl.DeviceIdType.MESH
    mine = lax.axis_index("dev")
    rank = lax.axis_index("half") * groups + lax.axis_index("grp")
    pairs = devs // 2
    pair, parity = mine // 2, mine % 2
    levels = (halves * groups).bit_length() - 1
    rows, p = panel_ref.shape
    n = trailing_ref.shape[1]
    blocks = p // NB

    def slot(dev):
        return pl.ds(pl.multiple_of(dev * rows, rows), rows)

    def same(step):
        return ((pair + step) % pairs) * 2 + parity

    def at_rank(level):
        bit = 1 << level
        other = rank + bit * (1 - 2 * ((rank // bit) % 2))
        return {"half": other // groups, "grp": other % groups}

    beside = pair * 2 + 1 - parity
    peers = [{"dev": same(step)} for step in range(1, pairs)] + [{"dev": beside}]
    peers += [at_rank(level) for level in range(levels)]
    barrier = pltpu.get_barrier_semaphore()
    for peer in peers:
        pl.semaphore_signal(barrier, inc=1, device_id=peer, device_id_type=mesh_ids)
    pl.semaphore_wait(barrier, len(peers))

    first = [
        pltpu.make_async_remote_copy(
            src_ref=panel_ref, dst_ref=panel.at[slot(mine)], send_sem=a_send.at[step],
            recv_sem=a_recv.at[step], device_id={"dev": same(step)}, device_id_type=mesh_ids)
        for step in range(1, pairs)
    ]
    onward = []
    for step in range(pairs):
        owner = same(pairs - step)
        onward.append(pltpu.make_async_remote_copy(
            src_ref=panel.at[slot(owner)] if step else panel_ref,
            dst_ref=panel.at[slot(owner)], send_sem=b_send.at[step],
            recv_sem=b_recv.at[step], device_id={"dev": beside}, device_id_type=mesh_ids))
    for copy in first:
        copy.start()
    onward[0].start()
    panel[slot(mine), :] = panel_ref[...]
    for step in range(1, pairs):
        first[step - 1].wait_recv()
        onward[step].start()
    for copy in onward:
        copy.wait_recv()

    where = packing(p, n)
    for i in range(blocks):
        left = panel[:, i * NB:(i + 1) * NB]
        strip = dot_t(left, panel[:, i * NB:p])
        for j in range(i, blocks):
            at = where[i, j]
            total[at:at + NB, :] = strip[:, (j - i) * NB:(j - i + 1) * NB]
    crossed = dot_t(panel[...], trailing_ref[...])
    for i in range(blocks):
        for j in range(n // NB):
            at = where[i, blocks + j]
            total[at:at + NB, :] = crossed[i * NB:(i + 1) * NB, j * NB:(j + 1) * NB]

    half = total.shape[0] // 2
    low = (rank % 2) * half
    keep = pl.ds(pl.multiple_of(low, 8), half)
    give = pl.ds(pl.multiple_of(half - low, 8), half)
    for level in range(levels):
        copy = pltpu.make_async_remote_copy(
            src_ref=total.at[keep if level else give], dst_ref=inbox.at[level],
            send_sem=r_send.at[level], recv_sem=r_recv.at[level],
            device_id=at_rank(level), device_id_type=mesh_ids)
        copy.start()
        if level == 0:
            group_ref[...] = panel[...]
        copy.wait()
        total[keep, :] += inbox[level]
    back = pltpu.make_async_remote_copy(
        src_ref=total.at[keep], dst_ref=inbox.at[levels],
        send_sem=r_send.at[levels], recv_sem=r_recv.at[levels],
        device_id=at_rank(0), device_id_type=mesh_ids)
    back.start()
    packed_ref[keep, :] = total[keep, :]
    for copy in first + onward:
        copy.wait_send()
    back.wait()
    packed_ref[give, :] = inbox[levels]


def gather_reduce(mesh, panel_block, trailing):
    halves, groups, devs = (mesh.shape[name] for name in ("half", "grp", "dev"))
    rows, p = panel_block.shape
    n = trailing.shape[1]
    f32 = jnp.float32
    size = len(packing(p, n)) * NB
    levels = (halves * groups).bit_length() - 1
    vmem = pl.BlockSpec(memory_space=pltpu.VMEM)
    dma = pltpu.SemaphoreType.DMA
    return pl.pallas_call(
        functools.partial(gather_kernel, halves, groups, devs),
        out_shape=(
            jax.ShapeDtypeStruct((rows * devs, p), f32),
            jax.ShapeDtypeStruct((size, NB), f32),
        ),
        in_specs=[vmem] * 2,
        out_specs=(vmem,) * 2,
        scratch_shapes=[
            pltpu.VMEM((rows * devs, p), f32),
            pltpu.VMEM((size, NB), f32),
            pltpu.VMEM((levels + 1, size // 2, NB), f32),
            dma((devs // 2,)), dma((devs // 2,)), dma((devs // 2,)), dma((devs // 2,)),
            dma((levels + 1,)), dma((levels + 1,)),
        ],
        compiler_params=pltpu.CompilerParams(collective_id=0, has_side_effects=True),
        name="gather_reduce",
    )(panel_block, trailing)


def on_device(mesh, panel_block, trailing):
    panel_group, packed = gather_reduce(mesh, panel_block, trailing)
    return solve(panel_group, packed, trailing)


def solution(mesh):
    placed = (P(("half", "grp", "dev"), None), P(("half", "grp"), "dev"))
    return jax.shard_map(
        functools.partial(on_device, mesh),
        mesh=mesh,
        in_specs=placed,
        out_specs=(P(), P(None, "dev"), P(("half", "grp"), "dev")),
        check_vma=False,
    )
```

profile of v0, /device:TPU:0, one launch (start us, length us, event | category | flops | bytes accessed | tf_op | source)
XLA Modules:
  0.0 68.5 jit_solution(11981074846333295825)
XLA Ops:
  0.6 42.7 %gather_reduce.1 = (f32[512,512]{1,0:T(8,128)}, f32[1792,128]{1,0:T(8,128)}) custom-call(f32[64,512]{1,0:T(8,128)} %panel_ref.1, f32[512,128]{1,0:T(8,128)} %trailing_ref.3), custom_call_target="tpu_custom_call" | custom-call | tf_op jit(solution)/shard_map/gather_reduce/pallas_call | solution.py:264
  43.3 25.2 %factor_project.1 = (f32[512,512]{1,0:T(8,128)}, f32[512,128]{1,0:T(8,128)}, f32[512,128]{1,0:T(8,128)}) custom-call(f32[512,512]{1,0:T(8,128)} %get-tuple-element.5.panel_ref, f32[1792,128]{1,0:T(8,128)} %get-tuple-element.6.packed_ref, f32[512,128]{1,0:T(8,128)} %trailing_ref.3), custom_call_target="tpu_custom_call" | custom-call | tf_op jit(solution)/shard_map/factor_project/pallas_call | solution.py:128
where the time goes:
time: 68.7 us; the launch traced here: 68.5 us
  Pallas kernels  67.9 us (99%)
    pallas_call x1, Pallas kernels, gather_reduce(): pl.pallas_call(functools.partial(gather_kernel, halves, groups, devs), ou...  42.7 us
    pallas_call x1, Pallas kernels, solve(): pl.pallas_call(solve_kernel, out_shape=(jax.ShapeDtypeStruct((p, p), f32)...  25.2 us

commit v1 on v0

v1 whole, which is shorter than its diff:
```python
import functools

import jax
import jax.numpy as jnp
from jax import lax
from jax.experimental import pallas as pl
from jax.experimental.pallas import tpu as pltpu
from jax.sharding import PartitionSpec as P

NB = 128
SUB = 8
PAIR = 2
F32 = jnp.float32
BF16 = jnp.bfloat16
LEFT = (0, 0, 1, 0, 1, 2)
RIGHT = (0, 1, 0, 2, 1, 0)


def split(x):
    high = x.astype(BF16)
    rest = x - high.astype(F32)
    middle = rest.astype(BF16)
    low = (rest - middle.astype(F32)).astype(BF16)
    return high, middle, low


def wide(parts, which, axis):
    return jnp.concatenate([parts[s] for s in which], axis=axis)


def contract(a, b, dim):
    return lax.dot_general(a, b, (((1,), (dim,)), ((), ())), preferred_element_type=F32)


def mm(a, b):
    return contract(wide(a, LEFT, 1), wide(b, RIGHT, 0), 0)


def mm_nt(a, b):
    return contract(wide(a, LEFT, 1), wide(b, RIGHT, 1), 1)


def lanes_of(x, at):
    return jnp.take_along_axis(x, jnp.full(x.shape, at, jnp.int32), axis=1)


def factor_block(block, upper_ref, inverse_ref, row0, col0, hook):
    tile = (SUB, NB)
    lane = lax.broadcasted_iota(jnp.int32, tile, 1)
    row = lax.broadcasted_iota(jnp.int32, tile, 0)
    here = [row == j for j in range(SUB)]
    block = list(block)
    groups = len(block)
    ups, lows = [], []
    for b in range(groups):
        hook(b)
        c0 = SUB * b
        own = block[b]
        near = min(groups, (b // PAIR + 2) * PAIR)
        inside = (lane >= c0) & (lane < c0 + SUB)
        cols = [lanes_of(own, c0 + t) for t in range(SUB)]
        columns = {g: [lanes_of(block[g], c0 + t) for t in range(SUB)] for g in range(b + 1, near)}
        v = jnp.where(inside, jnp.where(lane == row + c0, 1.0, 0.0), own)
        w = own
        up = low = None
        for j in range(SUB):
            top = [jnp.broadcast_to(cols[t][j:j + 1, :], tile) if t >= j else None
                   for t in range(SUB)]
            rs = lax.rsqrt(top[j])
            r = rs * rs
            e = cols[j] * r
            vj = jnp.broadcast_to(v[j:j + 1, :], tile)
            wj = jnp.broadcast_to(w[j:j + 1, :], tile)
            vs, ws = vj * rs, wj * rs
            up = ws if j == 0 else jnp.where(here[j], ws, up)
            low = vs if j == 0 else jnp.where(here[j], vs, low)
            v = jnp.where(here[j], vj * r, v - e * vj)
            if j + 1 < SUB:
                w = w - e * wj
            for t in range(j + 1, SUB):
                cols[t] = jnp.where(here[j], top[t] * r, cols[t] - (cols[j] * top[t]) * r)
        up = jnp.where(lane >= row + c0, up, 0.0)
        low = jnp.where(lane <= row + c0, low, 0.0)
        upper_ref[row0 + c0:row0 + c0 + SUB, col0:col0 + NB] = up
        inverse_ref[row0 + c0:row0 + c0 + SUB, :] = low
        ups.append(up)
        lows.append(low)
        if b + 1 < near:
            vt = [jnp.broadcast_to(v[t:t + 1, :], tile) for t in range(SUB)]
        for g in range(b + 1, near):
            terms = [columns[g][t] * vt[t] for t in range(SUB)]
            while len(terms) > 1:
                terms = [terms[i] + terms[i + 1] for i in range(0, len(terms), 2)]
            block[g] = jnp.where(inside, 0.0, block[g]) - terms[0]
        if (b + 1) % PAIR == 0 and near < groups:
            end = c0 + SUB
            past = lane >= end
            us = jnp.concatenate([jnp.where(past, u, 0.0) for u in ups[-PAIR:]], axis=0)
            vs = jnp.concatenate(
                [jnp.where(past, u, x) for u, x in zip(ups[-PAIR:], lows[-PAIR:])], axis=0)
            res = lax.dot_general(
                wide(split(us), LEFT, 0), wide(split(vs), RIGHT, 0), (((0,), (0,)), ((), ())),
                preferred_element_type=F32)
            done = (lane >= end - PAIR * SUB) & (lane < end)
            for g in range(near, groups):
                block[g] = jnp.where(done, 0.0, block[g]) - res[SUB * g:SUB * (g + 1), :]


def packing(p, n):
    blocks = p // NB
    where, stretch = {}, []
    at = 0
    for j in range(blocks):
        first = at
        for i in range(j + 1):
            where["gram", i, j] = at
            at += NB
        for i in ((j,) if j > 1 else (0, 1) if j == 1 else (0,) if blocks == 1 else ()):
            for q in range(n // NB):
                where["cross", i, q] = at
                at += NB
        stretch.append((first, at - first))
    return where, stretch, at


def fused_kernel(halves, groups, devs, panel_hbm, trailing_hbm, triangle_ref, projected_ref,
                 remainder_ref, panel, slab, total, inbox, work, inverse, panel3, turned3, slab3,
                 upper3, upper_t3, inverse3, inverse_t3, projected3, both3, y3,
                 l_sem, a_send, a_recv, b_send, b_recv, r_send, r_recv):
    mesh_ids = pl.DeviceIdType.MESH
    mine = lax.axis_index("dev")
    rank = lax.axis_index("half") * groups + lax.axis_index("grp")
    pairs = devs // 2
    pair, parity = mine // 2, mine % 2
    levels = (halves * groups).bit_length() - 1
    blocks, size, _ = panel.shape
    rows = size // devs
    p = blocks * NB
    n = slab.shape[1]
    last = blocks - 1
    where, stretch, _ = packing(p, n)

    def slot(dev):
        return pl.ds(pl.multiple_of(dev * rows, rows), rows)

    def same(step):
        return ((pair + step) % pairs) * 2 + parity

    def at_rank(level):
        bit = 1 << level
        other = rank + bit * (1 - 2 * ((rank // bit) % 2))
        return {"half": other // groups, "grp": other % groups}

    def blk(i):
        return slice(i * NB, (i + 1) * NB)

    loads = [pltpu.make_async_copy(panel_hbm.at[:, blk(j)], panel.at[j, slot(mine)], l_sem.at[j])
             for j in range(blocks)]
    loads.append(pltpu.make_async_copy(trailing_hbm, slab, l_sem.at[blocks]))
    for copy in loads:
        copy.start()

    beside = pair * 2 + 1 - parity
    peers = [{"dev": same(step)} for step in range(1, pairs)] + [{"dev": beside}]
    peers += [at_rank(level) for level in range(levels)]
    barrier = pltpu.get_barrier_semaphore()
    for peer in peers:
        pl.semaphore_signal(barrier, inc=1, device_id=peer, device_id_type=mesh_ids)
    pl.semaphore_wait(barrier, len(peers))

    first, onward = {}, {}
    for j in range(blocks):
        for step in range(1, pairs):
            first[j, step] = pltpu.make_async_remote_copy(
                src_ref=panel.at[j, slot(mine)], dst_ref=panel.at[j, slot(mine)],
                send_sem=a_send.at[j, step], recv_sem=a_recv.at[j, step],
                device_id={"dev": same(step)}, device_id_type=mesh_ids)
        for step in range(pairs):
            owner = same(pairs - step)
            onward[j, step] = pltpu.make_async_remote_copy(
                src_ref=panel.at[j, slot(owner)], dst_ref=panel.at[j, slot(owner)],
                send_sem=b_send.at[j, step], recv_sem=b_recv.at[j, step],
                device_id={"dev": beside}, device_id_type=mesh_ids)
    for j in range(blocks):
        loads[j].wait()
        for step in range(1, pairs):
            first[j, step].start()
        onward[j, 0].start()

    def forward(j):
        for step in range(1, pairs):
            first[j, step].wait_recv()
            onward[j, step].start()

    def reduction(j, level):
        begin, count = stretch[j]
        half = count // 2
        low = begin + (rank % 2) * half
        keep = pl.ds(pl.multiple_of(low, 8), half)
        give = pl.ds(pl.multiple_of(2 * begin + half - low, 8), half)
        copy = pltpu.make_async_remote_copy(
            src_ref=total.at[keep if level else give],
            dst_ref=inbox.at[level, pl.ds(begin // 2, half)],
            send_sem=r_send.at[level, j], recv_sem=r_recv.at[level, j],
            device_id=at_rank(level if level < levels else 0), device_id_type=mesh_ids)
        return copy, keep, give, slice(begin // 2, begin // 2 + half)

    def arrive(j):
        for step in range(pairs):
            onward[j, step].wait_recv()

    def prepare(j):
        x = panel[j]
        for s, part in enumerate(split(x)):
            panel3[s, j] = part
        for s, part in enumerate(split(x.T)):
            turned3[s, blk(j), :] = part

    def products(i, j):
        at = where["gram", i, j]
        total[at:at + NB, :] = mm([turned3[s, blk(i), :] for s in range(3)],
                                  [panel3[s, j] for s in range(3)])

    def crossed(i):
        out = mm([turned3[s, blk(i), :] for s in range(3)], [slab3[s] for s in range(3)])
        for q in range(n // NB):
            at = where["cross", i, q]
            total[at:at + NB, :] = out[:, blk(q)]

    def gram(j):
        prepare(j)
        for i in range(j + 1):
            products(i, j)
        if j > 1:
            crossed(j)
        elif j == 1:
            crossed(1)
        elif blocks == 1:
            load_slab()
            crossed(0)

    def load_slab():
        loads[blocks].wait()
        for s, part in enumerate(split(slab[...])):
            slab3[s] = part

    def begin(j):
        arrive(j)
        gram(j)
        reduction(j, 0)[0].start()
        if j == 0 and blocks > 1:
            load_slab()
            crossed(0)

    def advance(j, level):
        copy, keep, give, place = reduction(j, level)
        copy.wait()
        if level < levels:
            total[keep, :] += inbox[level, place]
            reduction(j, level + 1)[0].start()
        else:
            total[give, :] = inbox[level, place]

    queue = []
    for j in range(blocks):
        queue.append((2 * j, j, functools.partial(begin, j), None))
        for level in range(levels + 1):
            queue.append((2 * j + 1 + level, j, functools.partial(advance, j, level),
                          j if level == levels else None))
    for j in range(1, blocks):
        queue.append((2 * j - 1.5 if j < 3 else 2 * j - 2.5, j, functools.partial(forward, j), None))
    queue = [(task, end) for _, _, task, end in sorted(queue, key=lambda x: x[:2])]
    ready = set()

    def pump():
        if queue:
            task, end = queue.pop(0)
            task()
            if end is not None:
                ready.add(end)

    def ensure(j):
        while j not in ready:
            pump()

    def gram_of(i, j):
        at = where["gram", i, j]
        return total[at:at + NB, :]

    def cross_of(i):
        pieces = [where["cross", i, q] for q in range(n // NB)]
        return jnp.concatenate([total[at:at + NB, :] for at in pieces], axis=1)

    def put(ref, at, x):
        for s, part in enumerate(split(x)):
            ref[(s, *at)] = part

    def get(ref, *at):
        return [ref[(s, *at)] for s in range(3)]

    def lead(i, j):
        a = gram_of(i, j)
        if i:
            a = a - mm(get(upper_t3, blk(i), slice(0, i * NB)), get(upper3, slice(0, i * NB), blk(j)))
        return a

    def link(a, i, j):
        right = mm(get(inverse3, blk(i)), a[0])
        turned = mm_nt(a[1], get(inverse3, blk(i)))
        triangle_ref[blk(i), blk(j)] = right
        put(upper3, (blk(i), blk(j)), right)
        put(upper_t3, (blk(j), blk(i)), turned)

    def diagonal(j):
        if not j:
            return gram_of(0, 0)
        past = slice(0, j * NB)
        return gram_of(j, j) - mm(get(upper_t3, blk(j), past), get(upper3, past, blk(j)))

    def projection(j):
        d = cross_of(j)
        if j:
            past = slice(0, j * NB)
            d = d - mm(get(upper_t3, blk(j), past), get(projected3, past))
        return d

    forward(0)
    for i in range(1, blocks):
        triangle_ref[blk(i), 0:i * NB] = jnp.zeros((NB, i * NB), F32)

    def project(j):
        out = mm(get(inverse3, blk(j)), split(projection(j)))
        projected_ref[blk(j), :] = out
        put(projected3, (blk(j),), out)

    def back_substitution():
        for k in reversed(range(last)):
            rhs = jnp.concatenate([projected_ref[blk(k), :], triangle_ref[blk(k), blk(last)]], axis=1)
            if k + 1 < last:
                after = slice((k + 1) * NB, last * NB)
                rhs = rhs - mm(get(upper3, blk(k), after), get(both3, after))
            put(both3, (blk(k),), mm(get(inverse_t3, blk(k)), split(rhs)))

    def reduce_rest():
        rest = jnp.concatenate([slab[...], panel[last]], axis=1)
        if last:
            before = [jnp.concatenate([panel3[s, k] for k in range(last)], axis=1) for s in range(3)]
            rest = rest - mm(before, get(both3, slice(0, last * NB)))
        remainder_ref[...] = rest[:, 0:n]
        put(y3, (), rest[:, n:n + NB])

    for j in range(blocks):
        ensure(j)
        if j:
            for i in range(j):
                if (i, j) not in ready:
                    a = lead(i, j)
                    link((split(a), split(a.T)), i, j)
        work[...] = diagonal(j)
        tasks = []
        if j:
            tasks.append(functools.partial(project, j - 1))
        if j == last:
            tasks += [back_substitution, reduce_rest]

        def hook(b):
            if b and b % 2 == 0:
                pump()
            if b == 1:
                for task in tasks:
                    task()

        factor_block([work[SUB * g:SUB * (g + 1), :] for g in range(NB // SUB)],
                     triangle_ref, inverse, j * NB, j * NB, hook)
        done = inverse[blk(j), :]
        put(inverse3, (blk(j),), done)
        put(inverse_t3, (blk(j),), done.T)
    project(last)
    short = mm(get(inverse_t3, blk(last)), get(projected3, blk(last)))
    remainder_ref[...] = remainder_ref[...] - mm(get(y3), split(short))
    for copy in (*first.values(), *onward.values()):
        copy.wait_send()


def on_device(mesh, panel_block, trailing):
    halves, groups, devs = (mesh.shape[name] for name in ("half", "grp", "dev"))
    rows, p = panel_block.shape
    size, n = trailing.shape
    blocks = p // NB
    _, _, length = packing(p, n)
    levels = (halves * groups).bit_length() - 1
    vmem, dma = pltpu.VMEM, pltpu.SemaphoreType.DMA
    space = pl.BlockSpec(memory_space=pl.ANY)
    inside = pl.BlockSpec(memory_space=pltpu.VMEM)
    return pl.pallas_call(
        functools.partial(fused_kernel, halves, groups, devs),
        out_shape=(
            jax.ShapeDtypeStruct((p, p), F32),
            jax.ShapeDtypeStruct((p, n), F32),
            jax.ShapeDtypeStruct((size, n), F32),
        ),
        in_specs=[space] * 2,
        out_specs=(inside,) * 3,
        scratch_shapes=[
            vmem((blocks, size, NB), F32),
            vmem((size, n), F32),
            vmem((length, NB), F32),
            vmem((levels + 1, length // 2, NB), F32),
            vmem((NB, NB), F32),
            vmem((p, NB), F32),
            vmem((3, blocks, size, NB), BF16),
            vmem((3, p, size), BF16),
            vmem((3, size, n), BF16),
            vmem((3, p, p), BF16),
            vmem((3, p, p), BF16),
            vmem((3, p, NB), BF16),
            vmem((3, p, NB), BF16),
            vmem((3, p, n), BF16),
            vmem((3, p, n + NB), BF16),
            vmem((3, size, NB), BF16),
            dma((blocks + 1,)),
            dma((blocks, devs // 2)), dma((blocks, devs // 2)),
            dma((blocks, devs // 2)), dma((blocks, devs // 2)),
            dma((levels + 1, blocks)), dma((levels + 1, blocks)),
        ],
        compiler_params=pltpu.CompilerParams(collective_id=0, has_side_effects=True),
        name="factor_project",
    )(panel_block, trailing)


def solution(mesh):
    placed = (P(("half", "grp", "dev"), None), P(("half", "grp"), "dev"))
    return jax.shard_map(
        functools.partial(on_device, mesh),
        mesh=mesh,
        in_specs=placed,
        out_specs=(P(), P(None, "dev"), P(("half", "grp"), "dev")),
        check_vma=False,
    )
```

time: 68.7 us -> 62.4 us (0.908)
  Pallas kernels: 67.9 us -> 57.5 us
  local copies, waits for them, and re-layouts: 0 us -> 4.05 us
    pallas_call x2 -> x1, Pallas kernels: 67.9 us -> 57.5 us  [on_device(): pl.pallas_call(functools.partial(fused_kernel, halves, groups, devs), out...]
    unnamed x0 -> x7, local copies, waits for them, and re-layouts: none -> 4.05 us
where the time goes in v1:
time: 62.4 us; the launch traced here: 62.2 us
  Pallas kernels  57.5 us (92%)
  local copies, waits for them, and re-layouts  4.05 us (6%)
  between operations  0.65 us (1%)
    pallas_call x1, Pallas kernels, on_device(): pl.pallas_call(functools.partial(fused_kernel, halves, groups, devs), out...  57.5 us
    unnamed x7, local copies, waits for them, and re-layouts  4.05 us

profile of v1, /device:TPU:0, one launch (start us, length us, event | category | flops | bytes accessed | tf_op | source)
XLA Modules:
  0.0 62.2 jit_solution(5321262541417247414)
XLA Ops:
  0.6 57.5 %factor_project.1 = (f32[512,512]{1,0:T(8,128)}, f32[512,128]{1,0:T(8,128)}, f32[512,128]{1,0:T(8,128)}) custom-call(f32[64,512]{1,0:T(8,128)} %panel_hbm.1, f32[512,128]{1,0:T(8,128)} %trailing_hbm.1), custom_call_target="tpu_custom_call" | custom-call | tf_op jit(solution)/shard_map/factor_project/pallas_call | solution.py:395
  58.1 0.0 copy-start.1
  58.2 2.3 %copy.8 = f32[512,512]{1,0:T(8,128)} copy(f32[512,512]{1,0:T(8,128)} %get-tuple-element.6) | data formatting | bytes 2097152
  60.5 0.0 copy-done.1
  60.5 0.0 copy-start
  60.5 0.7 %copy.9 = f32[512,128]{1,0:T(8,128)} copy(f32[512,128]{1,0:T(8,128)S(1)} %copy-done.1) | data formatting | bytes 524288
  61.2 0.3 copy-done
  61.5 0.7 %copy.10 = f32[512,128]{1,0:T(8,128)} copy(f32[512,128]{1,0:T(8,128)S(1)} %copy-done) | data formatting | bytes 524288
Async XLA Ops:
  58.1 2.3 %copy-start.1 = (f32[512,128]{1,0:T(8,128)S(1)}, f32[512,128]{1,0:T(8,128)}, u32[]{:S(2)}) copy-start(f32[512,128]{1,0:T(8,128)} %get-tuple-element.7) | copy-start | bytes 786436
  60.5 1.0 %copy-start = (f32[512,128]{1,0:T(8,128)S(1)}, f32[512,128]{1,0:T(8,128)}, u32[]{:S(2)}) copy-start(f32[512,128]{1,0:T(8,128)} %get-tuple-element.8) | copy-start | bytes 786436

commit v2 on v1

--- a/solution.py
+++ b/solution.py
@@ -14,6 +14,18 @@
 BF16 = jnp.bfloat16
 LEFT = (0, 0, 1, 0, 1, 2)
 RIGHT = (0, 1, 0, 2, 1, 0)
+
+
+TIMES = {
+    ("gram", 0): (12.5, 14.6, 17.3, 18.3),
+    ("gram", 1): (16.6, 18.7, 21.4, 22.1),
+    ("cross", 1): (19.0, 19.9, 23.4, 24.2),
+    ("gram", 2): (20.4, 22.0, 25.9, 26.6),
+    ("gram", 3): (23.1, 24.6, 29.4, 30.2),
+    ("cross", 2): (24.9, 25.7, 30.0, 30.6),
+    ("cross", 3): (27.5, 28.3, 30.9, 31.5),
+}
+BEGINS = (18.6, 23.0, 27.0, 31.5)
 
 
 def split(x):
@@ -108,18 +120,21 @@
 
 def packing(p, n):
     blocks = p // NB
-    where, stretch = {}, []
+    regions = [("gram", (0,))]
+    for j in range(1, blocks):
+        regions.append(("gram", (j,)))
+        regions.append(("cross", (0, 1) if j == 1 else (j,)))
+    if blocks == 1:
+        regions.append(("cross", (0,)))
+    where, stretch = {}, {}
     at = 0
-    for j in range(blocks):
+    for kind, members in regions:
         first = at
-        for i in range(j + 1):
-            where["gram", i, j] = at
-            at += NB
-        for i in ((j,) if j > 1 else (0, 1) if j == 1 else (0,) if blocks == 1 else ()):
-            for q in range(n // NB):
-                where["cross", i, q] = at
+        for j in members:
+            for i in range(j + 1 if kind == "gram" else n // NB):
+                where[(kind, i, j) if kind == "gram" else (kind, j, i)] = at
                 at += NB
-        stretch.append((first, at - first))
+        stretch[kind, members[-1]] = (first, at - first)
     return where, stretch, at
 
 
@@ -185,15 +200,21 @@
         loads[j].wait()
         for step in range(1, pairs):
             first[j, step].start()
-        onward[j, 0].start()
+        if j < 2:
+            onward[j, 0].start()
 
     def forward(j):
         for step in range(1, pairs):
             first[j, step].wait_recv()
             onward[j, step].start()
-
-    def reduction(j, level):
-        begin, count = stretch[j]
+        if j + 2 < blocks:
+            onward[j + 2, 0].start()
+
+    names = list(stretch)
+
+    def reduction(name, level):
+        begin, count = stretch[name]
+        which = names.index(name)
         half = count // 2
         low = begin + (rank % 2) * half
         keep = pl.ds(pl.multiple_of(low, 8), half)
@@ -201,7 +222,7 @@
         copy = pltpu.make_async_remote_copy(
             src_ref=total.at[keep if level else give],
             dst_ref=inbox.at[level, pl.ds(begin // 2, half)],
-            send_sem=r_send.at[level, j], recv_sem=r_recv.at[level, j],
+            send_sem=r_send.at[level, which], recv_sem=r_recv.at[level, which],
             device_id=at_rank(level if level < levels else 0), device_id_type=mesh_ids)
         return copy, keep, give, slice(begin // 2, begin // 2 + half)
 
@@ -227,61 +248,52 @@
             at = where["cross", i, q]
             total[at:at + NB, :] = out[:, blk(q)]
 
-    def gram(j):
+    def begin_gram(j):
+        arrive(j)
         prepare(j)
         for i in range(j + 1):
             products(i, j)
-        if j > 1:
-            crossed(j)
-        elif j == 1:
-            crossed(1)
-        elif blocks == 1:
-            load_slab()
-            crossed(0)
-
-    def load_slab():
-        loads[blocks].wait()
-        for s, part in enumerate(split(slab[...])):
-            slab3[s] = part
-
-    def begin(j):
-        arrive(j)
-        gram(j)
-        reduction(j, 0)[0].start()
-        if j == 0 and blocks > 1:
-            load_slab()
-            crossed(0)
-
-    def advance(j, level):
-        copy, keep, give, place = reduction(j, level)
+        reduction(("gram", j), 0)[0].start()
+
+    def begin_cross(j):
+        if j < 2:
+            loads[blocks].wait()
+            for s, part in enumerate(split(slab[...])):
+                slab3[s] = part
+        for i in range(0 if j < 2 else j, j + 1):
+            crossed(i)
+        reduction(("cross", j), 0)[0].start()
+
+    def advance(name, level):
+        copy, keep, give, place = reduction(name, level)
         copy.wait()
         if level < levels:
             total[keep, :] += inbox[level, place]
-            reduction(j, level + 1)[0].start()
+            reduction(name, level + 1)[0].start()
         else:
             total[give, :] = inbox[level, place]
+            ready.add(name)
 
     queue = []
-    for j in range(blocks):
-        queue.append((2 * j, j, functools.partial(begin, j), None))
+    for j in range(1, blocks):
+        queue.append((12.4 + 3.0 * (j - 1), functools.partial(forward, j)))
+    for name in names:
+        first_at, *at = TIMES.get(name, (30.0, 31.0, 32.0, 33.0))
+        begin = begin_gram if name[0] == "gram" else begin_cross
+        queue.append((first_at, functools.partial(begin, name[1])))
         for level in range(levels + 1):
-            queue.append((2 * j + 1 + level, j, functools.partial(advance, j, level),
-                          j if level == levels else None))
-    for j in range(1, blocks):
-        queue.append((2 * j - 1.5 if j < 3 else 2 * j - 2.5, j, functools.partial(forward, j), None))
-    queue = [(task, end) for _, _, task, end in sorted(queue, key=lambda x: x[:2])]
+            place = 0 if level == 0 else 2 if level == levels else 1
+            queue.append((at[place], functools.partial(advance, name, level)))
+    queue.sort(key=lambda x: x[0])
     ready = set()
 
-    def pump():
-        if queue:
-            task, end = queue.pop(0)
-            task()
-            if end is not None:
-                ready.add(end)
-
-    def ensure(j):
-        while j not in ready:
-            pump()
+    def pump(until):
+        while queue and queue[0][0] <= until:
+            queue.pop(0)[1]()
+
+    def ensure(name):
+        while name not in ready:
+            queue.pop(0)[1]()
 
     def gram_of(i, j):
         at = where["gram", i, j]
@@ -333,15 +345,13 @@
         projected_ref[blk(j), :] = out
         put(projected3, (blk(j),), out)
 
-    def back_substitution():
+    def reduce_rest():
         for k in reversed(range(last)):
             rhs = jnp.concatenate([projected_ref[blk(k), :], triangle_ref[blk(k), blk(last)]], axis=1)
             if k + 1 < last:
                 after = slice((k + 1) * NB, last * NB)
                 rhs = rhs - mm(get(upper3, blk(k), after), get(both3, after))
             put(both3, (blk(k),), mm(get(inverse_t3, blk(k)), split(rhs)))
-
-    def reduce_rest():
         rest = jnp.concatenate([slab[...], panel[last]], axis=1)
         if last:
             before = [jnp.concatenate([panel3[s, k] for k in range(last)], axis=1) for s in range(3)]
@@ -349,32 +359,33 @@
         remainder_ref[...] = rest[:, 0:n]
         put(y3, (), rest[:, n:n + NB])
 
+    def project_at(i):
+        ensure(("cross", max(i, min(1, last))))
+        project(i)
+
     for j in range(blocks):
-        ensure(j)
-        if j:
-            for i in range(j):
-                if (i, j) not in ready:
-                    a = lead(i, j)
-                    link((split(a), split(a.T)), i, j)
+        ensure(("gram", j))
+        for i in range(j):
+            a = lead(i, j)
+            link((split(a), split(a.T)), i, j)
         work[...] = diagonal(j)
-        tasks = []
-        if j:
-            tasks.append(functools.partial(project, j - 1))
-        if j == last:
-            tasks += [back_substitution, reduce_rest]
 
         def hook(b):
-            if b and b % 2 == 0:
-                pump()
-            if b == 1:
-                for task in tasks:
-                    task()
+            pump(BEGINS[min(j, 3)] + 0.2 * b)
+            if j == last:
+                if b == 1:
+                    if j:
+                        project_at(j - 1)
+                    reduce_rest()
+            elif j and b == 11 - 8 * (j > 1):
+                project_at(j - 1)
 
         factor_block([work[SUB * g:SUB * (g + 1), :] for g in range(NB // SUB)],
                      triangle_ref, inverse, j * NB, j * NB, hook)
         done = inverse[blk(j), :]
         put(inverse3, (blk(j),), done)
         put(inverse_t3, (blk(j),), done.T)
+    ensure(("cross", last))
     project(last)
     short = mm(get(inverse_t3, blk(last)), get(projected3, blk(last)))
     remainder_ref[...] = remainder_ref[...] - mm(get(y3), split(short))
@@ -387,7 +398,7 @@
     rows, p = panel_block.shape
     size, n = trailing.shape
     blocks = p // NB
-    _, _, length = packing(p, n)
+    _, stretch, length = packing(p, n)
     levels = (halves * groups).bit_length() - 1
     vmem, dma = pltpu.VMEM, pltpu.SemaphoreType.DMA
     space = pl.BlockSpec(memory_space=pl.ANY)
@@ -395,9 +406,9 @@
     return pl.pallas_call(
         functools.partial(fused_kernel, halves, groups, devs),
         out_shape=(
-            jax.ShapeDtypeStruct((p, p), F32),
-            jax.ShapeDtypeStruct((p, n), F32),
-            jax.ShapeDtypeStruct((size, n), F32),
+            pltpu.VMEM((p, p), F32),
+            pltpu.VMEM((p, n), F32),
+            pltpu.VMEM((size, n), F32),
         ),
         in_specs=[space] * 2,
         out_specs=(inside,) * 3,
@@ -421,7 +432,7 @@
             dma((blocks + 1,)),
             dma((blocks, devs // 2)), dma((blocks, devs // 2)),
             dma((blocks, devs // 2)), dma((blocks, devs // 2)),
-            dma((levels + 1, blocks)), dma((levels + 1, blocks)),
+            dma((levels + 1, len(stretch))), dma((levels + 1, len(stretch))),
         ],
         compiler_params=pltpu.CompilerParams(collective_id=0, has_side_effects=True),
         name="factor_project",

time: 62.4 us -> 49 us (0.79)
  Pallas kernels: 57.5 us -> 45.8 us
  local copies, waits for them, and re-layouts: 4.05 us -> 2.38 us
    pallas_call x1, Pallas kernels: 57.5 us -> 45.8 us  [on_device(): pl.pallas_call(functools.partial(fused_kernel, halves, groups, devs), out...]
    unnamed x7 -> x3, local copies, waits for them, and re-layouts: 4.05 us -> 2.38 us
where the time goes in v2:
time: 49 us; the launch traced here: 48.8 us
  Pallas kernels  45.8 us (93%)
  local copies, waits for them, and re-layouts  2.38 us (5%)
  between operations  0.64 us (1%)
    pallas_call x1, Pallas kernels, on_device(): pl.pallas_call(functools.partial(fused_kernel, halves, groups, devs), out...  45.8 us
    unnamed x3, local copies, waits for them, and re-layouts  2.38 us

profile of v2, /device:TPU:0, one launch (start us, length us, event | category | flops | bytes accessed | tf_op | source)
XLA Modules:
  0.0 48.8 jit_solution(4915537336002507466)
XLA Ops:
  0.6 45.8 %factor_project.1 = (f32[512,512]{1,0:T(8,128)S(1)}, f32[512,128]{1,0:T(8,128)S(1)}, f32[512,128]{1,0:T(8,128)S(1)}) custom-call(f32[64,512]{1,0:T(8,128)} %panel_hbm.1, f32[512,128]{1,0:T(8,128)} %trailing_hbm.1), custom_call_target="tpu_custom_call" | custom-call | tf_op jit(solution)/shard_map/factor_project/pallas_call | solution.py:406
  46.4 1.0 %copy.8 = f32[512,512]{1,0:T(8,128)} copy(f32[512,512]{1,0:T(8,128)S(1)} %get-tuple-element.3) | data formatting | bytes 2097152
  47.4 0.7 %copy.9 = f32[512,128]{1,0:T(8,128)} copy(f32[512,128]{1,0:T(8,128)S(1)} %get-tuple-element.4) | data formatting | bytes 524288
  48.1 0.7 %copy.10 = f32[512,128]{1,0:T(8,128)} copy(f32[512,128]{1,0:T(8,128)S(1)} %get-tuple-element.5) | data formatting | bytes 524288

commit v3 on v2

v3 whole, which is shorter than its diff:
```python
import functools

import jax
import jax.numpy as jnp
from jax import lax
from jax.experimental import pallas as pl
from jax.experimental.pallas import tpu as pltpu
from jax.sharding import PartitionSpec as P

NB = 128
SUB = 8
PAIR = 2
F32 = jnp.float32
BF16 = jnp.bfloat16
LEFT = (0, 0, 1, 0, 1, 2)
RIGHT = (0, 1, 0, 2, 1, 0)


PLACES = {
    ("gram", 0): ((-12, -12), -10, -7, -5),
    ("gram", 1): ((-6, -6), 4, 15.3, 15.5),
    ("cross", 1): ((1,), 8, 18, 23),
    ("gram", 2): ((6, 7), 14, 23, 26),
    ("gram", 3): ((15.1, 15.2), 19, 36, 40),
    ("cross", 2): ((28,), 31.2, 45, 47.8),
    ("cross", 3): ((33,), 37, 47.6, 47.9),
}
FORWARDS = (0, -11, -9, 0)


def split(x):
    high = x.astype(BF16)
    rest = x - high.astype(F32)
    middle = rest.astype(BF16)
    low = (rest - middle.astype(F32)).astype(BF16)
    return high, middle, low


def wide(parts, which, axis):
    return jnp.concatenate([parts[s] for s in which], axis=axis)


def contract(a, b, dim):
    return lax.dot_general(a, b, (((1,), (dim,)), ((), ())), preferred_element_type=F32)


def mm(a, b):
    return contract(wide(a, LEFT, 1), wide(b, RIGHT, 0), 0)


def mm_nt(a, b):
    return contract(wide(a, LEFT, 1), wide(b, RIGHT, 1), 1)


def lanes_of(x, at):
    return jnp.take_along_axis(x, jnp.full(x.shape, at, jnp.int32), axis=1)


def factor_block(block, upper_ref, inverse_ref, row0, col0, hook):
    tile = (SUB, NB)
    lane = lax.broadcasted_iota(jnp.int32, tile, 1)
    row = lax.broadcasted_iota(jnp.int32, tile, 0)
    here = [row == j for j in range(SUB)]
    block = list(block)
    groups = len(block)
    ups, lows = [], []
    following = None

    def one(x, at):
        return jnp.broadcast_to(x[at:at + 1, :], tile)

    for b in range(groups):
        hook(b)
        c0 = SUB * b
        own = block[b]
        near = min(groups, (b // PAIR + 2) * PAIR)
        inside = (lane >= c0) & (lane < c0 + SUB)
        opens = b % PAIR == 0
        cols = [lanes_of(own, c0 + t) for t in range(SUB)] if opens else following
        columns = {g: [lanes_of(block[g], c0 + t) for t in range(SUB)] for g in range(b + 1, near)}
        if opens:
            following = [lanes_of(block[b + 1], c0 + SUB + t) for t in range(SUB)]
            below = list(columns[b + 1])
        v = jnp.where(inside, jnp.where(lane == row + c0, 1.0, 0.0), own)
        w = own
        up = low = None
        raw = list(cols)
        for j in range(SUB):
            top = [one(raw[t], j) if t >= j else None for t in range(SUB)]
            rs = lax.rsqrt(top[j])
            r = rs * rs
            e = cols[j] * r
            vj, wj = one(v, j), one(w, j)
            vs, ws = vj * rs, wj * rs
            up = ws if j == 0 else jnp.where(here[j], ws, up)
            low = vs if j == 0 else jnp.where(here[j], vs, low)
            v = jnp.where(here[j], vj * r, v - e * vj)
            if j + 1 < SUB:
                w = w - e * wj
            for t in range(j + 1, SUB):
                raw[t] = cols[t] - (cols[j] * top[t]) * r
                cols[t] = jnp.where(here[j], top[t] * r, raw[t])
            if opens:
                share = below[j] * r
                for t in range(SUB):
                    following[t] = following[t] - share * one(below[j], t)
                for t in range(j + 1, SUB):
                    below[t] = below[t] - (below[j] * top[t]) * r
        up = jnp.where(lane >= row + c0, up, 0.0)
        low = jnp.where(lane <= row + c0, low, 0.0)
        upper_ref[row0 + c0:row0 + c0 + SUB, col0:col0 + NB] = up
        inverse_ref[row0 + c0:row0 + c0 + SUB, :] = low
        ups.append(up)
        lows.append(low)
        if b + 1 < near:
            vt = [one(v, t) for t in range(SUB)]
        for g in range(b + 1, near):
            terms = [columns[g][t] * vt[t] for t in range(SUB)]
            while len(terms) > 1:
                terms = [terms[i] + terms[i + 1] for i in range(0, len(terms), 2)]
            block[g] = jnp.where(inside, 0.0, block[g]) - terms[0]
        if not opens and near < groups:
            end = c0 + SUB
            past = lane >= end
            us = jnp.concatenate([jnp.where(past, u, 0.0) for u in ups[-PAIR:]], axis=0)
            vs = jnp.concatenate(
                [jnp.where(past, u, x) for u, x in zip(ups[-PAIR:], lows[-PAIR:])], axis=0)
            res = lax.dot_general(
                wide(split(us), LEFT, 0), wide(split(vs), RIGHT, 0), (((0,), (0,)), ((), ())),
                preferred_element_type=F32)
            done = (lane >= end - PAIR * SUB) & (lane < end)
            for g in range(near, groups):
                block[g] = jnp.where(done, 0.0, block[g]) - res[SUB * g:SUB * (g + 1), :]


def packing(p, n):
    blocks = p // NB
    regions = [("gram", (0,))]
    for j in range(1, blocks):
        regions.append(("gram", (j,)))
        regions.append(("cross", (0, 1) if j == 1 else (j,)))
    if blocks == 1:
        regions.append(("cross", (0,)))
    where, stretch = {}, {}
    at = 0
    for kind, members in regions:
        first = at
        for j in members:
            for i in range(j + 1 if kind == "gram" else n // NB):
                where[(kind, i, j) if kind == "gram" else (kind, j, i)] = at
                at += NB
        stretch[kind, members[-1]] = (first, at - first)
    return where, stretch, at


def fused_kernel(halves, groups, devs, panel_hbm, trailing_hbm, triangle_ref, projected_ref,
                 remainder_ref, panel, slab, total, inbox, work, ahead3, inverse, panel3, turned3, slab3,
                 upper3, upper_t3, inverse3, inverse_t3, projected3, both3, y3, last3,
                 l_sem, s_sem, a_recv, b_recv, r_send, r_recv):
    mesh_ids = pl.DeviceIdType.MESH
    mine = lax.axis_index("dev")
    rank = lax.axis_index("half") * groups + lax.axis_index("grp")
    pairs = devs // 2
    pair, parity = mine // 2, mine % 2
    levels = (halves * groups).bit_length() - 1
    blocks, size, _ = panel.shape
    rows = size // devs
    p = blocks * NB
    n = slab.shape[1]
    last = blocks - 1
    where, stretch, _ = packing(p, n)

    def slot(dev):
        return pl.ds(pl.multiple_of(dev * rows, rows), rows)

    def same(step):
        return ((pair + step) % pairs) * 2 + parity

    def at_rank(level):
        bit = 1 << level
        other = rank + bit * (1 - 2 * ((rank // bit) % 2))
        return {"half": other // groups, "grp": other % groups}

    def blk(i):
        return slice(i * NB, (i + 1) * NB)

    for j in range(blocks):
        pltpu.make_async_copy(panel_hbm.at[:, blk(j)], panel.at[j, slot(mine)], l_sem.at[0]).start()
    slab_load = pltpu.make_async_copy(trailing_hbm, slab, l_sem.at[1])
    slab_load.start()

    beside = pair * 2 + 1 - parity
    peers = [{"dev": same(step)} for step in range(1, pairs)] + [{"dev": beside}]
    peers += [at_rank(level) for level in range(levels)]
    barrier = pltpu.get_barrier_semaphore()
    for peer in peers:
        pl.semaphore_signal(barrier, inc=1, device_id=peer, device_id_type=mesh_ids)
    pl.semaphore_wait(barrier, len(peers))

    def arrival(j, step):
        return pltpu.make_async_remote_copy(
            src_ref=panel.at[j, slot(mine)], dst_ref=panel.at[j, slot(mine)],
            send_sem=s_sem.at[0], recv_sem=a_recv.at[j, step - 1],
            device_id={"dev": same(step)}, device_id_type=mesh_ids)

    def passing(j, step):
        owner = same(pairs - step)
        return pltpu.make_async_remote_copy(
            src_ref=panel.at[j, slot(owner)], dst_ref=panel.at[j, slot(owner)],
            send_sem=s_sem.at[1], recv_sem=b_recv.at[j],
            device_id={"dev": beside}, device_id_type=mesh_ids)

    def send(j):
        if j < blocks:
            for step in range(1, pairs):
                arrival(j, step).start()

    own = panel.at[:, slot(mine)]
    pltpu.make_async_copy(own, own, l_sem.at[0]).wait()
    send(0)
    passing(0, 0).start()

    def forward(j):
        near = jnp.minimum(pair, pairs - 1 - pair)
        far = jnp.where(pair < pairs - 1 - pair, 1, -1)
        for k in range(pairs - 1):
            offset = jnp.where(k < 2 * near, (k // 2 + 1) * (1 - 2 * (k % 2)), (k - near + 1) * far)
            step = (pairs - offset) % pairs
            arrival(j, step).wait_recv()
            passing(j, step).start()
            if j == 0 and k == 0:
                send(1)
        send(j + 2)
        if j + 1 < blocks:
            passing(j + 1, 0).start()

    names = list(stretch)

    def reduction(name, level):
        begin, count = stretch[name]
        which = names.index(name)
        half = count // 2
        low = begin + (rank % 2) * half
        keep = pl.ds(pl.multiple_of(low, 8), half)
        give = pl.ds(pl.multiple_of(2 * begin + half - low, 8), half)
        copy = pltpu.make_async_remote_copy(
            src_ref=total.at[keep if level else give],
            dst_ref=inbox.at[level, pl.ds(begin // 2, half)],
            send_sem=r_send.at[level, which], recv_sem=r_recv.at[level, which],
            device_id=at_rank(level if level < levels else 0), device_id_type=mesh_ids)
        return copy, keep, give, slice(begin // 2, begin // 2 + half)

    def together(part, which, at):
        return pltpu.make_async_remote_copy(
            src_ref=part, dst_ref=part, send_sem=s_sem.at[which], recv_sem=b_recv.at[at],
            device_id={"dev": beside}, device_id_type=mesh_ids)

    def arrive(j):
        together(panel.at[j, pl.ds(0, pairs * rows)], 1, j).wait_recv()

    def prepare(j):
        x = panel[j]
        for s, part in enumerate(split(x)):
            panel3[s, j] = part
        for s, part in enumerate(split(x.T)):
            turned3[s, blk(j), :] = part

    def products(j):
        at = where["gram", 0, j]
        total[at:at + (j + 1) * NB, :] = mm([turned3[s, 0:(j + 1) * NB, :] for s in range(3)],
                                            [panel3[s, j] for s in range(3)])

    def crossed(i):
        out = mm([turned3[s, blk(i), :] for s in range(3)], [slab3[s] for s in range(3)])
        for q in range(n // NB):
            at = where["cross", i, q]
            total[at:at + NB, :] = out[:, blk(q)]

    def begin(name):
        reduction(name, 0)[0].start()

    def receive(j):
        arrive(j)
        prepare(j)

    def load_slab():
        slab_load.wait()
        for s, part in enumerate(split(slab[...])):
            slab3[s] = part

    def advance(name, level):
        copy, keep, give, place = reduction(name, level)
        copy.wait()
        if level < levels:
            total[keep, :] += inbox[level, place]
            reduction(name, level + 1)[0].start()
        else:
            total[give, :] = inbox[level, place]
            ready.add(name)

    queue = []

    def add(place, task, *args):
        queue.append((place, functools.partial(task, *args)))

    for j in range(1, blocks):
        add(FORWARDS[min(j, 3)], forward, j)
    for name in names:
        kind, j = name
        start, *at = PLACES.get(name, ((48, 48), 49, 50, 51))
        if kind == "gram":
            add(start[0], receive, j)
            add(start[1], products, j)
        elif j < 2:
            add(-8.5, load_slab)
            add(-8.5, crossed, 0)
        if kind == "cross" and j:
            add(start[0], crossed, j)
        add(start[-1], begin, name)
        for level in range(levels + 1):
            add(at[0 if level == 0 else 2 if level == levels else 1], advance, name, level)
    ready = set()

    def pump(place):
        while queue and queue[0][0] <= place:
            queue.pop(0)[1]()

    def ensure(name):
        at = 0
        while name not in ready:
            while queue[at][1].func is need:
                at += 1
            queue.pop(at)[1]()

    def gram_of(i, j):
        at = where["gram", i, j]
        return total[at:at + NB, :]

    def cross_of(i):
        pieces = [where["cross", i, q] for q in range(n // NB)]
        return jnp.concatenate([total[at:at + NB, :] for at in pieces], axis=1)

    def put(ref, at, x):
        for s, part in enumerate(split(x)):
            ref[(s, *at)] = part

    def get(ref, *at):
        return [ref[(s, *at)] for s in range(3)]

    def lead(i, j):
        a = gram_of(i, j)
        if i:
            a = a - mm(get(upper_t3, blk(i), slice(0, i * NB)), get(upper3, slice(0, i * NB), blk(j)))
        return a

    def link(i, j, a, turned):
        right = mm(get(inverse3, blk(i)), a)
        turned = mm_nt(turned, get(inverse3, blk(i)))
        triangle_ref[blk(i), blk(j)] = right
        put(upper3, (blk(i), blk(j)), right)
        put(upper_t3, (blk(j), blk(i)), turned)

    def early_link(i, j):
        a = lead(i, j)
        link(i, j, split(a), split(a.T))

    def early(j):
        i = j - 1
        a = lead(i, j)
        put(ahead3, (0,), a)
        put(ahead3, (1,), a.T)
        d = gram_of(j, j)
        if i:
            past = slice(0, i * NB)
            d = d - mm(get(upper_t3, blk(j), past), get(upper3, past, blk(j)))
        work[...] = d

    def late(j):
        i = j - 1
        link(i, j, get(ahead3, 0), get(ahead3, 1))
        work[...] -= mm(get(upper_t3, blk(j), blk(i)), get(upper3, blk(i), blk(j)))

    def projection(j):
        d = cross_of(j)
        if j:
            past = slice(0, j * NB)
            d = d - mm(get(upper_t3, blk(j), past), get(projected3, past))
        return d

    forward(0)
    for i in range(1, blocks):
        triangle_ref[blk(i), 0:i * NB] = jnp.zeros((NB, i * NB), F32)

    def project(j):
        out = mm(get(inverse3, blk(j)), split(projection(j)))
        projected_ref[blk(j), :] = out
        put(projected3, (blk(j),), out)

    def solve_back(k):
        rhs = jnp.concatenate([projected_ref[blk(k), :], triangle_ref[blk(k), blk(last)]], axis=1)
        if k + 1 < last:
            after = slice((k + 1) * NB, last * NB)
            rhs = rhs - mm(get(upper3, blk(k), after), get(both3, after))
        put(both3, (blk(k),), mm(get(inverse_t3, blk(k)), split(rhs)))

    def reduce_rest(at):
        rest = jnp.concatenate([slab[at, :], panel[last, at, :]], axis=1)
        if last:
            before = [jnp.concatenate([panel3[s, k, at, :] for k in range(last)], axis=1)
                      for s in range(3)]
            rest = rest - mm(before, get(both3, slice(0, last * NB)))
        remainder_ref[at, :] = rest[:, 0:n]
        put(y3, (at,), rest[:, n:n + NB])

    def need(task, names, *args):
        for name in names:
            ensure(name)
        task(*args)

    for j in range(1, blocks):
        for i in range(j - 1):
            add(16 * j + (-6 if j == 2 else -9) + 3 * i, need, early_link, [("gram", j)], i, j)
        add(16 * j - 1.5, need, early, [("gram", j)], j)
        name = ("cross", max(j - 1, min(1, last)))
        add(16 * j + (8 if j == 1 else 3 if j < last else 1), need, project, [name], j - 1)
    add(16 * last + 1.5, need, lambda: put(last3, (), projection(last)), [("cross", last)])
    for k in range(last):
        add(16 * last + 2 + 2 * k, solve_back, last - 1 - k)
    for r in range(0, size, NB):
        add(16 * last + 4 + 2 * last + 2 * (r // NB), reduce_rest, slice(r, r + NB))
    queue.sort(key=lambda x: x[0])

    for j in range(blocks):
        ensure(("gram", j))
        if j:
            pump(16 * j - 1)
            late(j)
        else:
            work[...] = gram_of(0, 0)
        factor_block([work[SUB * g:SUB * (g + 1), :] for g in range(NB // SUB)],
                     triangle_ref, inverse, j * NB, j * NB, lambda b: pump(16 * j + b))
        done = inverse[blk(j), :]
        put(inverse3, (blk(j),), done)
        if j < last:
            put(inverse_t3, (blk(j),), done.T)
    while queue:
        queue.pop(0)[1]()
    out = mm(get(inverse3, blk(last)), get(last3))
    projected_ref[blk(last), :] = out
    basis = mm_nt(get(y3), get(inverse3, blk(last)))
    remainder_ref[...] = remainder_ref[...] - mm(split(basis), split(out))
    together(panel.at[:, pl.ds(0, (pairs - 1) * rows)], 0, 0).wait_send()
    together(panel.at[:, pl.ds(0, pairs * rows)], 1, 0).wait_send()


def on_device(mesh, panel_block, trailing):
    halves, groups, devs = (mesh.shape[name] for name in ("half", "grp", "dev"))
    rows, p = panel_block.shape
    size, n = trailing.shape
    blocks = p // NB
    _, stretch, length = packing(p, n)
    levels = (halves * groups).bit_length() - 1
    vmem, dma = pltpu.VMEM, pltpu.SemaphoreType.DMA
    space = pl.BlockSpec(memory_space=pl.ANY)
    inside = pl.BlockSpec(memory_space=pltpu.VMEM)
    return pl.pallas_call(
        functools.partial(fused_kernel, halves, groups, devs),
        out_shape=(
            pltpu.VMEM((p, p), F32),
            pltpu.VMEM((p, n), F32),
            pltpu.VMEM((size, n), F32),
        ),
        in_specs=[space] * 2,
        out_specs=(inside,) * 3,
        scratch_shapes=[
            vmem((blocks, size, NB), F32),
            vmem((size, n), F32),
            vmem((length, NB), F32),
            vmem((levels + 1, length // 2, NB), F32),
            vmem((NB, NB), F32),
            vmem((3, 2, NB, NB), BF16),
            vmem((p, NB), F32),
            vmem((3, blocks, size, NB), BF16),
            vmem((3, p, size), BF16),
            vmem((3, size, n), BF16),
            vmem((3, p, p), BF16),
            vmem((3, p, p), BF16),
            vmem((3, p, NB), BF16),
            vmem((3, p, NB), BF16),
            vmem((3, p, n), BF16),
            vmem((3, p, n + NB), BF16),
            vmem((3, size, NB), BF16),
            vmem((3, NB, n), BF16),
            dma((2,)), dma((2,)), dma((blocks, devs // 2 - 1)), dma((blocks,)),
            dma((levels + 1, len(stretch))), dma((levels + 1, len(stretch))),
        ],
        compiler_params=pltpu.CompilerParams(collective_id=0, has_side_effects=True),
        name="factor_project",
    )(panel_block, trailing)


def solution(mesh):
    placed = (P(("half", "grp", "dev"), None), P(("half", "grp"), "dev"))
    return jax.shard_map(
        functools.partial(on_device, mesh),
        mesh=mesh,
        in_specs=placed,
        out_specs=(P(), P(None, "dev"), P(("half", "grp"), "dev")),
        check_vma=False,
    )
```

time: 49 us -> 45.4 us (0.927)
  Pallas kernels: 45.8 us -> 42.2 us
    pallas_call x1, Pallas kernels: 45.8 us -> 42.2 us  [on_device(): pl.pallas_call(functools.partial(fused_kernel, halves, groups, devs), out...]
where the time goes in v3:
time: 45.4 us; the launch traced here: 45.2 us
  Pallas kernels  42.2 us (93%)
  local copies, waits for them, and re-layouts  2.38 us (5%)
  between operations  0.64 us (1%)
    pallas_call x1, Pallas kernels, on_device(): pl.pallas_call(functools.partial(fused_kernel, halves, groups, devs), out...  42.2 us
    unnamed x3, local copies, waits for them, and re-layouts  2.38 us

profile of v3, /device:TPU:0, one launch (start us, length us, event | category | flops | bytes accessed | tf_op | source)
XLA Modules:
  0.0 45.2 jit_solution(15222870124188845634)
XLA Ops:
  0.6 42.2 %factor_project.1 = (f32[512,512]{1,0:T(8,128)S(1)}, f32[512,128]{1,0:T(8,128)S(1)}, f32[512,128]{1,0:T(8,128)S(1)}) custom-call(f32[64,512]{1,0:T(8,128)} %panel_hbm.1, f32[512,128]{1,0:T(8,128)} %trailing_hbm.1), custom_call_target="tpu_custom_call" | custom-call | tf_op jit(solution)/shard_map/factor_project/pallas_call | solution.py:466
  42.9 1.0 %copy.8 = f32[512,512]{1,0:T(8,128)} copy(f32[512,512]{1,0:T(8,128)S(1)} %get-tuple-element.3) | data formatting | bytes 2097152
  43.8 0.7 %copy.9 = f32[512,128]{1,0:T(8,128)} copy(f32[512,128]{1,0:T(8,128)S(1)} %get-tuple-element.4) | data formatting | bytes 524288
  44.5 0.7 %copy.10 = f32[512,128]{1,0:T(8,128)} copy(f32[512,128]{1,0:T(8,128)S(1)} %get-tuple-element.5) | data formatting | bytes 524288

commit v4 on v3

--- a/solution.py
+++ b/solution.py
@@ -18,13 +18,14 @@
 
 PLACES = {
     ("gram", 0): ((-12, -12), -10, -7, -5),
-    ("gram", 1): ((-6, -6), 4, 15.3, 15.5),
-    ("cross", 1): ((1,), 8, 18, 23),
-    ("gram", 2): ((6, 7), 14, 23, 26),
-    ("gram", 3): ((15.1, 15.2), 19, 36, 40),
-    ("cross", 2): ((28,), 31.2, 45, 47.8),
-    ("cross", 3): ((33,), 37, 47.6, 47.9),
+    ("gram", 1): ((-6, -6), 2, 15, 15.9),
+    ("cross", 1): ((2.1,), 9, 19, 23),
+    ("gram", 2): ((6, 7), 13, 24, 28),
+    ("gram", 3): ((14.5, 15.2), 18, 35, 39.5),
+    ("cross", 2): ((20,), 25, 40, 43),
+    ("cross", 3): ((21,), 28.5, 44, 47.9),
 }
+
 FORWARDS = (0, -11, -9, 0)
 
 
@@ -266,15 +267,15 @@
             turned3[s, blk(j), :] = part
 
     def products(j):
-        at = where["gram", 0, j]
-        total[at:at + (j + 1) * NB, :] = mm([turned3[s, 0:(j + 1) * NB, :] for s in range(3)],
-                                            [panel3[s, j] for s in range(3)])
-
-    def crossed(i):
-        out = mm([turned3[s, blk(i), :] for s in range(3)], [slab3[s] for s in range(3)])
+        right = [jnp.concatenate([*(panel3[s, i] for i in range(j + 1)), slab3[s]], axis=1)
+                 for s in range(3)]
+        out = mm([turned3[s, blk(j), :] for s in range(3)], right)
+        for i in range(j + 1):
+            at = where["gram", i, j]
+            total[at:at + NB, :] = out[:, blk(i)]
         for q in range(n // NB):
-            at = where["cross", i, q]
-            total[at:at + NB, :] = out[:, blk(q)]
+            at = where["cross", j, q]
+            total[at:at + NB, :] = out[:, blk(j + 1 + q)]
 
     def begin(name):
         reduction(name, 0)[0].start()
@@ -311,11 +312,6 @@
         if kind == "gram":
             add(start[0], receive, j)
             add(start[1], products, j)
-        elif j < 2:
-            add(-8.5, load_slab)
-            add(-8.5, crossed, 0)
-        if kind == "cross" and j:
-            add(start[0], crossed, j)
         add(start[-1], begin, name)
         for level in range(levels + 1):
             add(at[0 if level == 0 else 2 if level == levels else 1], advance, name, level)
@@ -350,8 +346,9 @@
     def lead(i, j):
         a = gram_of(i, j)
         if i:
-            a = a - mm(get(upper_t3, blk(i), slice(0, i * NB)), get(upper3, slice(0, i * NB), blk(j)))
-        return a
+            past = slice(0, i * NB)
+            a = a - mm(get(upper_t3, blk(j), past), get(upper3, past, blk(i)))
+        return a.T, a
 
     def link(i, j, a, turned):
         right = mm(get(inverse3, blk(i)), a)
@@ -361,14 +358,14 @@
         put(upper_t3, (blk(j), blk(i)), turned)
 
     def early_link(i, j):
-        a = lead(i, j)
-        link(i, j, split(a), split(a.T))
+        a, turned = lead(i, j)
+        link(i, j, split(a), split(turned))
 
     def early(j):
         i = j - 1
-        a = lead(i, j)
+        a, turned = lead(i, j)
         put(ahead3, (0,), a)
-        put(ahead3, (1,), a.T)
+        put(ahead3, (1,), turned)
         d = gram_of(j, j)
         if i:
             past = slice(0, i * NB)
@@ -387,6 +384,7 @@
             d = d - mm(get(upper_t3, blk(j), past), get(projected3, past))
         return d
 
+    load_slab()
     forward(0)
     for i in range(1, blocks):
         triangle_ref[blk(i), 0:i * NB] = jnp.zeros((NB, i * NB), F32)
@@ -419,7 +417,7 @@
 
     for j in range(1, blocks):
         for i in range(j - 1):
-            add(16 * j + (-6 if j == 2 else -9) + 3 * i, need, early_link, [("gram", j)], i, j)
+            add(16 * j + (-3 if j == 2 else -8) + 3 * i, need, early_link, [("gram", j)], i, j)
         add(16 * j - 1.5, need, early, [("gram", j)], j)
         name = ("cross", max(j - 1, min(1, last)))
         add(16 * j + (8 if j == 1 else 3 if j < last else 1), need, project, [name], j - 1)

time: 45.4 us -> 43.2 us (0.952)
  Pallas kernels: 42.2 us -> 40 us
    pallas_call x1, Pallas kernels: 42.2 us -> 40 us  [on_device(): pl.pallas_call(functools.partial(fused_kernel, halves, groups, devs), out...]
where the time goes in v4:
time: 43.2 us; the launch traced here: 43 us
  Pallas kernels  40 us (93%)
  local copies, waits for them, and re-layouts  2.38 us (6%)
  between operations  0.64 us (1%)
    pallas_call x1, Pallas kernels, on_device(): pl.pallas_call(functools.partial(fused_kernel, halves, groups, devs), out...  40 us
    unnamed x3, local copies, waits for them, and re-layouts  2.38 us

profile of v4, /device:TPU:0, one launch (start us, length us, event | category | flops | bytes accessed | tf_op | source)
XLA Modules:
  0.0 43.0 jit_solution(4761310847188675323)
XLA Ops:
  0.6 40.0 %factor_project.1 = (f32[512,512]{1,0:T(8,128)S(1)}, f32[512,128]{1,0:T(8,128)S(1)}, f32[512,128]{1,0:T(8,128)S(1)}) custom-call(f32[64,512]{1,0:T(8,128)} %panel_hbm.1, f32[512,128]{1,0:T(8,128)} %trailing_hbm.1), custom_call_target="tpu_custom_call" | custom-call | tf_op jit(solution)/shard_map/factor_project/pallas_call | solution.py:464
  40.7 1.0 %copy.8 = f32[512,512]{1,0:T(8,128)} copy(f32[512,512]{1,0:T(8,128)S(1)} %get-tuple-element.3) | data formatting | bytes 2097152
  41.6 0.7 %copy.9 = f32[512,128]{1,0:T(8,128)} copy(f32[512,128]{1,0:T(8,128)S(1)} %get-tuple-element.4) | data formatting | bytes 524288
  42.3 0.7 %copy.10 = f32[512,128]{1,0:T(8,128)} copy(f32[512,128]{1,0:T(8,128)S(1)} %get-tuple-element.5) | data formatting | bytes 524288

commit v5 on v4

--- a/solution.py
+++ b/solution.py
@@ -9,6 +9,7 @@
 
 NB = 128
 SUB = 8
+LIMIT = 24 << 20
 PAIR = 2
 F32 = jnp.float32
 BF16 = jnp.bfloat16
@@ -51,6 +52,19 @@
 
 def mm_nt(a, b):
     return contract(wide(a, LEFT, 1), wide(b, RIGHT, 1), 1)
+
+
+def blk(i):
+    return slice(i * NB, (i + 1) * NB)
+
+
+def put(ref, at, x):
+    for s, part in enumerate(split(x)):
+        ref[(s, *at)] = part
+
+
+def get(ref, *at):
+    return [ref[(s, *at)] for s in range(3)]
 
 
 def lanes_of(x, at):
@@ -154,10 +168,9 @@
     return where, stretch, at
 
 
-def fused_kernel(halves, groups, devs, panel_hbm, trailing_hbm, triangle_ref, projected_ref,
-                 remainder_ref, panel, slab, total, inbox, work, ahead3, inverse, panel3, turned3, slab3,
-                 upper3, upper_t3, inverse3, inverse_t3, projected3, both3, y3, last3,
-                 l_sem, s_sem, a_recv, b_recv, r_send, r_recv):
+def lead_kernel(halves, groups, devs, panel_hbm, trailing_hbm, triangle_ref, projected_ref, work,
+                total, panel, panel3, slab, upper3, upper_t3, inverse3, inverse_t3, projected3,
+                inbox, ahead3, inverse, turned3, slab3, l_sem, s_sem, a_recv, b_recv, r_send, r_recv):
     mesh_ids = pl.DeviceIdType.MESH
     mine = lax.axis_index("dev")
     rank = lax.axis_index("half") * groups + lax.axis_index("grp")
@@ -181,9 +194,6 @@
         bit = 1 << level
         other = rank + bit * (1 - 2 * ((rank // bit) % 2))
         return {"half": other // groups, "grp": other % groups}
-
-    def blk(i):
-        return slice(i * NB, (i + 1) * NB)
 
     for j in range(blocks):
         pltpu.make_async_copy(panel_hbm.at[:, blk(j)], panel.at[j, slot(mine)], l_sem.at[0]).start()
@@ -336,13 +346,6 @@
         pieces = [where["cross", i, q] for q in range(n // NB)]
         return jnp.concatenate([total[at:at + NB, :] for at in pieces], axis=1)
 
-    def put(ref, at, x):
-        for s, part in enumerate(split(x)):
-            ref[(s, *at)] = part
-
-    def get(ref, *at):
-        return [ref[(s, *at)] for s in range(3)]
-
     def lead(i, j):
         a = gram_of(i, j)
         if i:
@@ -394,22 +397,6 @@
         projected_ref[blk(j), :] = out
         put(projected3, (blk(j),), out)
 
-    def solve_back(k):
-        rhs = jnp.concatenate([projected_ref[blk(k), :], triangle_ref[blk(k), blk(last)]], axis=1)
-        if k + 1 < last:
-            after = slice((k + 1) * NB, last * NB)
-            rhs = rhs - mm(get(upper3, blk(k), after), get(both3, after))
-        put(both3, (blk(k),), mm(get(inverse_t3, blk(k)), split(rhs)))
-
-    def reduce_rest(at):
-        rest = jnp.concatenate([slab[at, :], panel[last, at, :]], axis=1)
-        if last:
-            before = [jnp.concatenate([panel3[s, k, at, :] for k in range(last)], axis=1)
-                      for s in range(3)]
-            rest = rest - mm(before, get(both3, slice(0, last * NB)))
-        remainder_ref[at, :] = rest[:, 0:n]
-        put(y3, (at,), rest[:, n:n + NB])
-
     def need(task, names, *args):
         for name in names:
             ensure(name)
@@ -419,13 +406,8 @@
         for i in range(j - 1):
             add(16 * j + (-3 if j == 2 else -8) + 3 * i, need, early_link, [("gram", j)], i, j)
         add(16 * j - 1.5, need, early, [("gram", j)], j)
-        name = ("cross", max(j - 1, min(1, last)))
-        add(16 * j + (8 if j == 1 else 3 if j < last else 1), need, project, [name], j - 1)
-    add(16 * last + 1.5, need, lambda: put(last3, (), projection(last)), [("cross", last)])
-    for k in range(last):
-        add(16 * last + 2 + 2 * k, solve_back, last - 1 - k)
-    for r in range(0, size, NB):
-        add(16 * last + 4 + 2 * last + 2 * (r // NB), reduce_rest, slice(r, r + NB))
+        if j < last:
+            add(16 * j + (8 if j == 1 else 3), need, project, [("cross", max(j - 1, 1))], j - 1)
     queue.sort(key=lambda x: x[0])
 
     for j in range(blocks):
@@ -435,20 +417,97 @@
             late(j)
         else:
             work[...] = gram_of(0, 0)
-        factor_block([work[SUB * g:SUB * (g + 1), :] for g in range(NB // SUB)],
-                     triangle_ref, inverse, j * NB, j * NB, lambda b: pump(16 * j + b))
-        done = inverse[blk(j), :]
-        put(inverse3, (blk(j),), done)
         if j < last:
+            factor_block([work[SUB * g:SUB * (g + 1), :] for g in range(NB // SUB)],
+                         triangle_ref, inverse, j * NB, j * NB, lambda b: pump(16 * j + b))
+            done = inverse[blk(j), :]
+            put(inverse3, (blk(j),), done)
             put(inverse_t3, (blk(j),), done.T)
     while queue:
         queue.pop(0)[1]()
-    out = mm(get(inverse3, blk(last)), get(last3))
-    projected_ref[blk(last), :] = out
-    basis = mm_nt(get(y3), get(inverse3, blk(last)))
-    remainder_ref[...] = remainder_ref[...] - mm(split(basis), split(out))
     together(panel.at[:, pl.ds(0, (pairs - 1) * rows)], 0, 0).wait_send()
     together(panel.at[:, pl.ds(0, pairs * rows)], 1, 0).wait_send()
+
+
+def last_kernel(triangle_in, projected_in, work, total, panel, panel3, slab, upper3, upper_t3,
+                inverse3, inverse_t3, projected3, triangle_ref, projected_ref, remainder_ref,
+                corner, inverse, projected, remainder, fresh3, both3, y3, last3, sems):
+    blocks, size, _ = panel.shape
+    n = slab.shape[1]
+    last = blocks - 1
+    where, _, _ = packing(blocks * NB, n)
+    copies = []
+
+    def send(source, target):
+        copies.append(pltpu.make_async_copy(source, target, sems.at[len(copies)]))
+        copies[-1].start()
+
+    send(triangle_in.at[0:last * NB], triangle_ref.at[0:last * NB])
+    send(triangle_in.at[blk(last), 0:last * NB], triangle_ref.at[blk(last), 0:last * NB])
+    if last > 1:
+        send(projected_in.at[0:(last - 1) * NB], projected_ref.at[0:(last - 1) * NB])
+
+    def projection(j, before):
+        pieces = [where["cross", j, q] for q in range(n // NB)]
+        d = jnp.concatenate([total[at:at + NB, :] for at in pieces], axis=1)
+        return d - mm(get(upper_t3, blk(j), slice(0, j * NB)), before) if j else d
+
+    def project():
+        j = last - 1
+        out = mm(get(inverse3, blk(j)), split(projection(j, get(projected3, slice(0, j * NB)))))
+        projected[blk(j), :] = out
+        put(fresh3, (), out)
+        send(projected.at[blk(j)], projected_ref.at[blk(j)])
+
+    def project_last():
+        j = last - 1
+        before = [jnp.concatenate([projected3[s, 0:j * NB], fresh3[s]], axis=0) if j else fresh3[s]
+                  for s in range(3)]
+        put(last3, (), projection(last, before))
+
+    def solve_back(k):
+        own = projected if k == last - 1 else projected_in
+        rhs = jnp.concatenate([own[blk(k), :], triangle_in[blk(k), blk(last)]], axis=1)
+        if k + 1 < last:
+            after = slice((k + 1) * NB, last * NB)
+            rhs = rhs - mm(get(upper3, blk(k), after), get(both3, after))
+        put(both3, (blk(k),), mm(get(inverse_t3, blk(k)), split(rhs)))
+
+    def reduce_rest(at):
+        rest = jnp.concatenate([slab[at, :], panel[last, at, :]], axis=1)
+        if last:
+            before = [jnp.concatenate([panel3[s, k, at, :] for k in range(last)], axis=1)
+                      for s in range(3)]
+            rest = rest - mm(before, get(both3, slice(0, last * NB)))
+        remainder[at, :] = rest[:, 0:n]
+        put(y3, (at,), rest[:, n:n + NB])
+
+    tasks = {}
+    if last:
+        tasks[1] = [project, project_last]
+    for k in range(last):
+        tasks.setdefault(2 + 2 * k, []).append(functools.partial(solve_back, last - 1 - k))
+    for r in range(0, size, NB):
+        tasks.setdefault(min(4 + 2 * last + 2 * (r // NB), 15), []).append(
+            functools.partial(reduce_rest, slice(r, r + NB)))
+    if not last:
+        put(last3, (), projection(0, None))
+
+    def hook(b):
+        for task in tasks.get(b, []):
+            task()
+
+    factor_block([work[SUB * g:SUB * (g + 1), :] for g in range(NB // SUB)], corner, inverse, 0, 0, hook)
+    send(corner, triangle_ref.at[blk(last), blk(last)])
+    done = split(inverse[...])
+    out = mm(done, get(last3))
+    projected[blk(last), :] = out
+    send(projected.at[blk(last)], projected_ref.at[blk(last)])
+    basis = mm_nt(get(y3), done)
+    remainder[...] = remainder[...] - mm(split(basis), split(out))
+    send(remainder, remainder_ref)
+    for copy in copies:
+        copy.wait()
 
 
 def on_device(mesh, panel_block, trailing):
@@ -461,40 +520,47 @@
     vmem, dma = pltpu.VMEM, pltpu.SemaphoreType.DMA
     space = pl.BlockSpec(memory_space=pl.ANY)
     inside = pl.BlockSpec(memory_space=pltpu.VMEM)
-    return pl.pallas_call(
-        functools.partial(fused_kernel, halves, groups, devs),
-        out_shape=(
-            pltpu.VMEM((p, p), F32),
-            pltpu.VMEM((p, n), F32),
-            pltpu.VMEM((size, n), F32),
-        ),
+    kept = (
+        vmem((p, p), F32), vmem((p, n), F32), vmem((NB, NB), F32), vmem((length, NB), F32),
+        vmem((blocks, size, NB), F32), vmem((3, blocks, size, NB), BF16), vmem((size, n), F32),
+        vmem((3, p, p), BF16), vmem((3, p, p), BF16), vmem((3, p, NB), BF16), vmem((3, p, NB), BF16),
+        vmem((3, p, n), BF16),
+    )
+    found = pl.pallas_call(
+        functools.partial(lead_kernel, halves, groups, devs),
+        out_shape=kept,
         in_specs=[space] * 2,
-        out_specs=(inside,) * 3,
+        out_specs=(inside,) * len(kept),
         scratch_shapes=[
-            vmem((blocks, size, NB), F32),
-            vmem((size, n), F32),
-            vmem((length, NB), F32),
             vmem((levels + 1, length // 2, NB), F32),
-            vmem((NB, NB), F32),
             vmem((3, 2, NB, NB), BF16),
             vmem((p, NB), F32),
-            vmem((3, blocks, size, NB), BF16),
             vmem((3, p, size), BF16),
             vmem((3, size, n), BF16),
-            vmem((3, p, p), BF16),
-            vmem((3, p, p), BF16),
-            vmem((3, p, NB), BF16),
-            vmem((3, p, NB), BF16),
-            vmem((3, p, n), BF16),
-            vmem((3, p, n + NB), BF16),
-            vmem((3, size, NB), BF16),
-            vmem((3, NB, n), BF16),
             dma((2,)), dma((2,)), dma((blocks, devs // 2 - 1)), dma((blocks,)),
             dma((levels + 1, len(stretch))), dma((levels + 1, len(stretch))),
         ],
-        compiler_params=pltpu.CompilerParams(collective_id=0, has_side_effects=True),
-        name="factor_project",
-    )(panel_block, trailing)
+        compiler_params=pltpu.CompilerParams(
+            collective_id=0, has_side_effects=True, vmem_limit_bytes=LIMIT),
+        name="lead_blocks",
+    )(*(pltpu.with_memory_space_constraint(x, pltpu.HBM) for x in (panel_block, trailing)))
+    return pl.pallas_call(
+        last_kernel,
+        out_shape=(
+            jax.ShapeDtypeStruct((p, p), F32),
+            jax.ShapeDtypeStruct((p, n), F32),
+            jax.ShapeDtypeStruct((size, n), F32),
+        ),
+        in_specs=[inside] * len(kept),
+        out_specs=(space,) * 3,
+        scratch_shapes=[
+            vmem((NB, NB), F32), vmem((NB, NB), F32), vmem((p, n), F32), vmem((size, n), F32),
+            vmem((3, NB, n), BF16), vmem((3, p, n + NB), BF16), vmem((3, size, NB), BF16),
+            vmem((3, NB, n), BF16), dma((7,)),
+        ],
+        compiler_params=pltpu.CompilerParams(vmem_limit_bytes=LIMIT),
+        name="last_block",
+    )(*(pltpu.with_memory_space_constraint(x, pltpu.VMEM) for x in found))
 
 
 def solution(mesh):

time: 43.2 us -> 41.5 us (0.961)
  local copies, waits for them, and re-layouts: 2.38 us -> 0 us
  Pallas kernels: 40 us -> 40.8 us
    unnamed x3 -> x0, local copies, waits for them, and re-layouts: 2.38 us -> none
    pallas_call x1 -> x2, Pallas kernels: 40 us -> 40.8 us  [the longest x1 35.7 us: on_device(): pl.pallas_call(functools.partial(lead_kernel, halves, groups, devs), out_...]
where the time goes in v5:
time: 41.5 us; the launch traced here: 41.4 us
  Pallas kernels  40.8 us (98%)
  between operations  0.64 us (2%)
    pallas_call x1, Pallas kernels, on_device(): pl.pallas_call(functools.partial(lead_kernel, halves, groups, devs), out_...  35.7 us
    pallas_call x1, Pallas kernels, on_device(): pl.pallas_call(last_kernel, out_shape=(jax.ShapeDtypeStruct((p, p), F32),...  5.02 us

profile of v5, /device:TPU:0, one launch (start us, length us, event | category | flops | bytes accessed | tf_op | source)
XLA Modules:
  0.0 41.4 jit_solution(9236998759193142300)
XLA Ops:
  0.6 35.7 %lead_blocks.1 = (f32[512,512]{1,0:T(8,128)S(1)}, f32[512,128]{1,0:T(8,128)S(1)}, f32[128,128]{1,0:T(8,128)S(1)}, f32[1792,128]{1,0:T(8,128)S(1)}, f32[4,512,128...) custom-call(f32[64,512]{1,0:T(8,128)} %panel_hbm.1, ...), custom_call_target="tpu_custom_call" | custom-call | tf_op jit(solution)/shard_map/lead_blocks/pallas_call | solution.py:529
  36.4 5.0 %last_block.1 = (f32[512,512]{1,0:T(8,128)}, f32[512,128]{1,0:T(8,128)}, f32[512,128]{1,0:T(8,128)}) custom-call(f32[512,512]{1,0:T(8,128)S(1)} %get-tuple-element.15.triangle_in, f32[512,128]{1,0:T(8,128)S(1)} %get-tuple-element.16.projected_in, f32[128,128]{1,0:T(8,128)S(1)} %get-tuple-element.17.work, f32[1792,128]{1,0:T(8,128)S(1)} %get-tuple-element.18.total, ...), custom_call_target="tpu_custom_call" | custom-call | tf_op jit(solution)/shard_map/last_block/pallas_call | solution.py:547

commit v6 on v5

--- a/solution.py
+++ b/solution.py
@@ -19,12 +19,12 @@
 
 PLACES = {
     ("gram", 0): ((-12, -12), -10, -7, -5),
-    ("gram", 1): ((-6, -6), 2, 15, 15.9),
-    ("cross", 1): ((2.1,), 9, 19, 23),
-    ("gram", 2): ((6, 7), 13, 24, 28),
-    ("gram", 3): ((14.5, 15.2), 18, 35, 39.5),
-    ("cross", 2): ((20,), 25, 40, 43),
-    ("cross", 3): ((21,), 28.5, 44, 47.9),
+    ("gram", 1): ((-6, -6), 2, 15.3, 15.9),
+    ("cross", 1): ((2.1,), 9, 22, 30),
+    ("gram", 2): ((6, 7), 13, 22.1, 28),
+    ("gram", 3): ((15, 15.4), 18, 38, 43),
+    ("cross", 2): ((20,), 31.2, 43.1, 47),
+    ("cross", 3): ((21,), 31.3, 43.2, 47.1),
 }
 
 FORWARDS = (0, -11, -9, 0)
@@ -404,10 +404,10 @@
 
     for j in range(1, blocks):
         for i in range(j - 1):
-            add(16 * j + (-3 if j == 2 else -8) + 3 * i, need, early_link, [("gram", j)], i, j)
+            add(16 * j + (-3 if j == 2 else -5) + 2 * i, need, early_link, [("gram", j)], i, j)
         add(16 * j - 1.5, need, early, [("gram", j)], j)
         if j < last:
-            add(16 * j + (8 if j == 1 else 3), need, project, [("cross", max(j - 1, 1))], j - 1)
+            add(16 * j + (15 if j == 1 else 4), need, project, [("cross", max(j - 1, 1))], j - 1)
     queue.sort(key=lambda x: x[0])
 
     for j in range(blocks):
@@ -503,9 +503,11 @@
     out = mm(done, get(last3))
     projected[blk(last), :] = out
     send(projected.at[blk(last)], projected_ref.at[blk(last)])
-    basis = mm_nt(get(y3), done)
-    remainder[...] = remainder[...] - mm(split(basis), split(out))
-    send(remainder, remainder_ref)
+    part = split(out)
+    for at in (slice(0, size // 2), slice(size // 2, size)):
+        basis = mm_nt(get(y3, at), done)
+        remainder[at, :] = remainder[at, :] - mm(split(basis), part)
+        send(remainder.at[at], remainder_ref.at[at])
     for copy in copies:
         copy.wait()
 
@@ -556,7 +558,7 @@
         scratch_shapes=[
             vmem((NB, NB), F32), vmem((NB, NB), F32), vmem((p, n), F32), vmem((size, n), F32),
             vmem((3, NB, n), BF16), vmem((3, p, n + NB), BF16), vmem((3, size, NB), BF16),
-            vmem((3, NB, n), BF16), dma((7,)),
+            vmem((3, NB, n), BF16), dma((8,)),
         ],
         compiler_params=pltpu.CompilerParams(vmem_limit_bytes=LIMIT),
         name="last_block",

time: 41.5 us -> 41 us (0.988)
  Pallas kernels: 40.8 us -> 40.2 us
where the time goes in v6:
time: 41 us; the launch traced here: 40.8 us
  Pallas kernels  40.2 us (98%)
  between operations  0.64 us (2%)
    pallas_call x1, Pallas kernels, on_device(): pl.pallas_call(functools.partial(lead_kernel, halves, groups, devs), out_...  35.4 us
    pallas_call x1, Pallas kernels, on_device(): pl.pallas_call(last_kernel, out_shape=(jax.ShapeDtypeStruct((p, p), F32),...  4.81 us

profile of v6, /device:TPU:0, one launch (start us, length us, event | category | flops | bytes accessed | tf_op | source)
XLA Modules:
  0.0 40.8 jit_solution(11462546461337465064)
XLA Ops:
  0.6 35.4 %lead_blocks.1 = (f32[512,512]{1,0:T(8,128)S(1)}, f32[512,128]{1,0:T(8,128)S(1)}, f32[128,128]{1,0:T(8,128)S(1)}, f32[1792,128]{1,0:T(8,128)S(1)}, f32[4,512,128...) custom-call(f32[64,512]{1,0:T(8,128)} %panel_hbm.1, ...), custom_call_target="tpu_custom_call" | custom-call | tf_op jit(solution)/shard_map/lead_blocks/pallas_call | solution.py:531
  36.0 4.8 %last_block.1 = (f32[512,512]{1,0:T(8,128)}, f32[512,128]{1,0:T(8,128)}, f32[512,128]{1,0:T(8,128)}) custom-call(f32[512,512]{1,0:T(8,128)S(1)} %get-tuple-element.15.triangle_in, f32[512,128]{1,0:T(8,128)S(1)} %get-tuple-element.16.projected_in, f32[128,128]{1,0:T(8,128)S(1)} %get-tuple-element.17.work, f32[1792,128]{1,0:T(8,128)S(1)} %get-tuple-element.18.total, ...), custom_call_target="tpu_custom_call" | custom-call | tf_op jit(solution)/shard_map/last_block/pallas_call | solution.py:549

commit v7 on v6

--- a/solution.py
+++ b/solution.py
@@ -19,8 +19,8 @@
 
 PLACES = {
     ("gram", 0): ((-12, -12), -10, -7, -5),
-    ("gram", 1): ((-6, -6), 2, 15.3, 15.9),
-    ("cross", 1): ((2.1,), 9, 22, 30),
+    ("gram", 1): ((-6, -6), 1, 15.3, 15.9),
+    ("cross", 1): ((1.1,), 5.5, 22, 30),
     ("gram", 2): ((6, 7), 13, 22.1, 28),
     ("gram", 3): ((15, 15.4), 18, 38, 43),
     ("cross", 2): ((20,), 31.2, 43.1, 47),
@@ -239,7 +239,7 @@
             step = (pairs - offset) % pairs
             arrival(j, step).wait_recv()
             passing(j, step).start()
-            if j == 0 and k == 0:
+            if j == 0 and k == 1:
                 send(1)
         send(j + 2)
         if j + 1 < blocks:

time: 41 us -> 40.3 us (0.983)
  Pallas kernels: 40.2 us -> 39.5 us
    pallas_call x1, Pallas kernels: 35.4 us -> 34.7 us  [on_device(): pl.pallas_call(functools.partial(lead_kernel, halves, groups, devs), out_...]
where the time goes in v7:
time: 40.3 us; the launch traced here: 40.1 us
  Pallas kernels  39.5 us (98%)
  between operations  0.64 us (2%)
    pallas_call x1, Pallas kernels, on_device(): pl.pallas_call(functools.partial(lead_kernel, halves, groups, devs), out_...  34.7 us
    pallas_call x1, Pallas kernels, on_device(): pl.pallas_call(last_kernel, out_shape=(jax.ShapeDtypeStruct((p, p), F32),...  4.81 us

profile of v7, /device:TPU:0, one launch (start us, length us, event | category | flops | bytes accessed | tf_op | source)
XLA Modules:
  0.0 40.1 jit_solution(2371068842886003269)
XLA Ops:
  0.6 34.7 %lead_blocks.1 = (f32[512,512]{1,0:T(8,128)S(1)}, f32[512,128]{1,0:T(8,128)S(1)}, f32[128,128]{1,0:T(8,128)S(1)}, f32[1792,128]{1,0:T(8,128)S(1)}, f32[4,512,128...) custom-call(f32[64,512]{1,0:T(8,128)} %panel_hbm.1, ...), custom_call_target="tpu_custom_call" | custom-call | tf_op jit(solution)/shard_map/lead_blocks/pallas_call | solution.py:531
  35.3 4.8 %last_block.1 = (f32[512,512]{1,0:T(8,128)}, f32[512,128]{1,0:T(8,128)}, f32[512,128]{1,0:T(8,128)}) custom-call(f32[512,512]{1,0:T(8,128)S(1)} %get-tuple-element.15.triangle_in, f32[512,128]{1,0:T(8,128)S(1)} %get-tuple-element.16.projected_in, f32[128,128]{1,0:T(8,128)S(1)} %get-tuple-element.17.work, f32[1792,128]{1,0:T(8,128)S(1)} %get-tuple-element.18.total, ...), custom_call_target="tpu_custom_call" | custom-call | tf_op jit(solution)/shard_map/last_block/pallas_call | solution.py:549

commit v8 on v7

--- a/solution.py
+++ b/solution.py
@@ -487,9 +487,9 @@
         tasks[1] = [project, project_last]
     for k in range(last):
         tasks.setdefault(2 + 2 * k, []).append(functools.partial(solve_back, last - 1 - k))
-    for r in range(0, size, NB):
+    for r in range(0, size, 2 * NB):
         tasks.setdefault(min(4 + 2 * last + 2 * (r // NB), 15), []).append(
-            functools.partial(reduce_rest, slice(r, r + NB)))
+            functools.partial(reduce_rest, slice(r, r + 2 * NB)))
     if not last:
         put(last3, (), projection(0, None))
 

time: 40.3 us -> 40.3 us (level)
  no operation moved by 1% of the time
where the time goes in v8:
time: 40.3 us; the launch traced here: 40.1 us
  Pallas kernels  39.5 us (98%)
  between operations  0.64 us (2%)
    pallas_call x1, Pallas kernels, on_device(): pl.pallas_call(functools.partial(lead_kernel, halves, groups, devs), out_...  34.7 us
    pallas_call x1, Pallas kernels, on_device(): pl.pallas_call(last_kernel, out_shape=(jax.ShapeDtypeStruct((p, p), F32),...  4.81 us

profile of v8, /device:TPU:0, one launch (start us, length us, event | category | flops | bytes accessed | tf_op | source)
XLA Modules:
  0.0 40.1 jit_solution(11151996998385574238)
XLA Ops:
  0.6 34.7 %lead_blocks.1 = (f32[512,512]{1,0:T(8,128)S(1)}, f32[512,128]{1,0:T(8,128)S(1)}, f32[128,128]{1,0:T(8,128)S(1)}, f32[1792,128]{1,0:T(8,128)S(1)}, f32[4,512,128...) custom-call(f32[64,512]{1,0:T(8,128)} %panel_hbm.1, ...), custom_call_target="tpu_custom_call" | custom-call | tf_op jit(solution)/shard_map/lead_blocks/pallas_call | solution.py:531
  35.3 4.8 %last_block.1 = (f32[512,512]{1,0:T(8,128)}, f32[512,128]{1,0:T(8,128)}, f32[512,128]{1,0:T(8,128)}) custom-call(f32[512,512]{1,0:T(8,128)S(1)} %get-tuple-element.15.triangle_in, f32[512,128]{1,0:T(8,128)S(1)} %get-tuple-element.16.projected_in, f32[128,128]{1,0:T(8,128)S(1)} %get-tuple-element.17.work, f32[1792,128]{1,0:T(8,128)S(1)} %get-tuple-element.18.total, ...), custom_call_target="tpu_custom_call" | custom-call | tf_op jit(solution)/shard_map/last_block/pallas_call | solution.py:549
